TPU v7x, 32 devices: a whole 2x2x4 slice. The times are simulated.
32 devices in a mesh: section: 2 (over core), dp: 16 (over z, y, x).
Axes of the slice: x: 2, y: 2, z: 4, core: 2. Of those that a mesh axis runs over, the one named last changes fastest.
Arguments:
- node_table: bfloat16 [128, 2048], replicated, may hold values from -60 to 60
- tiles: int32 [4, 512], P(None, 'dp'), may hold values from 0 to 96
- neighbours: int32 [4, 512, 8], P(None, 'dp'), may hold values from 0 to 31
- distances: float32 [4, 512, 8], P(None, 'dp'), may hold values from 0 to 0.9
- proj: bfloat16 [2, 2048, 512], P('section'), may hold values from -0.125 to 0.125
- upstream: bfloat16 [4, 512, 2048], P(None, 'dp'), may hold values from -6 to 6
Outputs:
- grad: float32 [2, 2048, 512], P('section', 'dp')
All inputs are finite; a program needn't handle non-finite values.
Results may differ from a plain program's by a relative error of at most 0.024.
Values may be sent and summed in bfloat16 or wider, within the bound.
No kernel may reach another device: no remote copies, remote signals or barrier semaphores. Data moves between devices by JAX's collectives and lax.ppermute only.
A program may use at most 64 MiB of HBM per device.

v0:
```python
import functools
import itertools
import math

import jax
import jax.numpy as jnp
from jax import lax
from jax.experimental import pallas as pl
from jax.experimental.pallas import tpu as pltpu
from jax.sharding import PartitionSpec as P


epsilon = 1e-05
AXES = ("section", "dp")
SHARED_BITS = (2, 0)
LIMIT = 36 << 20


def mask_of(number, bits):
    return sum(((number >> i) & 1) << bit for i, bit in enumerate(bits))


class Plan:
    def __init__(self, sections, replicas, points):
        self.sections, self.replicas, self.points = sections, replicas, points
        bits = replicas.bit_length() - 1
        self.shared = tuple(bit for bit in SHARED_BITS if bit < bits)
        self.summed = tuple(bit for bit in (1, 3, *range(bits)) if bit < bits and bit not in self.shared)
        self.summed = tuple(dict.fromkeys(self.summed))
        self.rows = (points << len(self.shared)) // sections
        self.unit = min(points, self.rows)
        self.units = self.rows // self.unit
        self.parts = points // self.unit
        self.blocks = 1 << len(self.summed)
        self.loads = 1 if sections == 2 else sections
        self.held = 2 if sections == 2 else 1
        self.relayed = sections == 2 and len(self.shared) == 2 and points % 32 == 0

    def order(self, section):
        turn = section % max(len(self.summed), 1)
        return self.summed[turn:] + self.summed[:turn]

    def units_of(self, section):
        units = [divmod(section * self.units + j, self.parts) for j in range(self.units)]
        units = [(mask_of(number, self.shared), part) for number, part in units]
        return sorted(units, key=lambda unit: unit[0].bit_count() != 1)

    def source_mask(self, section, j):
        return self.units_of(section)[j][0]


def permute(block, plan, route):
    pairs = []
    for section, replica in itertools.product(range(plan.sections), range(plan.replicas)):
        to_section, to_replica = route(section, replica)
        pairs.append((section * plan.replicas + replica, to_section * plan.replicas + to_replica))
    return lax.ppermute(block, AXES, pairs)


def dot(left, right, dims):
    return lax.dot_general(left, right, (dims, ((), ())), preferred_element_type=jnp.float32)


CHUNK = 256


def chunks(width):
    size = CHUNK if width % CHUNK == 0 else width
    return [pl.ds(start, size) for start in range(0, width, size)]


def lanes(value):
    size = value.shape[1]
    tile = 128 if size % 128 == 0 else size
    return sum(value[:, start : start + tile] for start in range(0, size, tile))


def by_section(plan, weights, body):
    me = lax.axis_index("section")
    if plan.sections != 2:
        body(me, lambda s: weights[0].at[s])
        return
    for place in range(2):
        pl.when(me == place)(functools.partial(body, place, lambda s, place=place: weights[(s + place) % 2]))


def prepare_kernel(plan, *refs):
    (*arrays, upstream), small, refs = refs[:4], refs[4], refs[5:]
    halves, (*held, sem) = (refs[:2], refs[2:]) if plan.relayed else ((), refs)
    packed = [pltpu.make_async_copy(array, ref, sem.at[j]) for j, (array, ref) in enumerate(zip(arrays, held))]
    taken = []
    half = plan.points // 2
    for j, ref in enumerate(halves):
        place = pl.multiple_of((lax.axis_index("section") ^ j) * half, half)
        taken.append(pltpu.make_async_copy(upstream.at[pl.ds(place, half)], ref, sem.at[3 + j]))
    for copy in packed + taken:
        copy.start()
    for copy in packed:
        copy.wait()
    tiles, neighbours, distances = held
    micro_count, near, _ = neighbours.shape
    index = [(neighbours[m] + tiles[m : m + 1, :]).astype(jnp.float32) for m in range(micro_count)]
    small[:near, :] = jnp.concatenate(index, axis=1)
    small[near:, :] = jnp.concatenate([distances[m] for m in range(micro_count)], axis=1)
    for copy in taken:
        copy.wait()


def load_kernel(plan, table, *refs):
    weights, refs = refs[: plan.loads], refs[plan.loads :]
    twice, held, sem = refs
    nodes = table.shape[0]
    copies = [pltpu.make_async_copy(table, twice.at[pl.ds(i * nodes, nodes)], sem.at[i]) for i in range(2)]
    if plan.sections == 2:
        copies.append(pltpu.make_async_copy(weights[0].at[0], held, sem.at[2]))
    else:
        me = lax.axis_index("section")
        for turn, weight in enumerate(weights):
            place = lax.rem(me + turn, plan.sections)
            copies.append(pltpu.make_async_copy(weight.at[0], held.at[place], sem.at[2 + turn]))
    for copy in copies:
        copy.start()
    for copy in copies:
        copy.wait()


def forward_kernel(plan, *refs):
    units, sections = plan.units, plan.sections
    given = 3 if plan.relayed else units
    small, twice, refs = refs[:given], refs[given], refs[given + 1 :]
    weights, refs = refs[: plan.held], refs[plan.held :]
    streams, hiddens, inputs, scales, total = refs
    nodes, width = twice.shape[0] // 2, twice.shape[1]
    rank = hiddens.shape[2]
    me = lax.axis_index("section")
    count = small[0].shape[0] // 2
    packed = [ref[...] for ref in small]
    if plan.relayed:
        half = plan.unit // 2
        near, across, own = packed
        low_half = lax.broadcasted_iota(jnp.int32, own.shape, 1) < half
        mixed = jnp.where(low_half == (me == 0), own, across)
        packed = [jnp.where(me == 0, a, b) for a, b in ((near, pltpu.roll(near, half, 1)), (pltpu.roll(mixed, half, 1), mixed))]
    selectors = []
    for j in range(units):
        index = packed[j][:count, :].astype(jnp.int32)
        distance = packed[j][count:, :]
        kernel = (1.0 - distance) ** 3 * (1.0 + 3.0 * distance)
        kernel = kernel / jnp.sum(kernel, axis=0, keepdims=True)
        node = lax.broadcasted_iota(jnp.int32, (nodes, plan.unit), 0)
        selector = jnp.zeros((nodes, plan.unit), jnp.float32)
        for k in range(count):
            selector += jnp.where(node == index[k : k + 1, :], kernel[k : k + 1, :], 0.0)
        high = selector.astype(jnp.bfloat16)
        low = (selector - high.astype(jnp.float32)).astype(jnp.bfloat16)
        selectors.append(jnp.concatenate([high, low], axis=0))
    selector = jnp.concatenate(selectors, axis=1) if units > 1 else selectors[0]
    squares = 0.0
    for columns in chunks(width):
        value = dot(selector, twice[:, columns], ((0,), (0,))).astype(jnp.bfloat16)
        streams[0, :, columns] = value
        value = value.astype(jnp.float32)
        squares += lanes(value * value)
    total[...] = squares

    def body(me, weight_of):
        squares = total[...]
        for s in range(sections):
            weight = weight_of(s)
            scale = lax.rsqrt(jnp.sum(squares, axis=1, keepdims=True) * (1.0 / width) + epsilon)
            scales[s] = jnp.broadcast_to(scale, scales.shape[1:])
            for columns in chunks(rank):
                value = dot(streams[s], weight[:, columns], ((1,), (0,))) * scale
                inputs[s, :, columns] = value
                hiddens[s, :, columns] = jnp.tanh(value).astype(jnp.bfloat16)
            if s + 1 == sections:
                break
            squares = 0.0
            for columns in chunks(width):
                value = streams[s, :, columns].astype(jnp.float32) + dot(hiddens[s], weight[columns, :], ((1,), (1,)))
                value = value.astype(jnp.bfloat16)
                streams[s + 1, :, columns] = value
                value = value.astype(jnp.float32)
                squares += lanes(value * value)

    by_section(plan, weights, body)


def backward_kernel(plan, *refs):
    sections = plan.sections
    given = 4 if plan.relayed else plan.units
    arrived, refs = refs[:given], refs[given:]
    streams, hiddens, inputs, scales = refs[:4]
    weights, refs = refs[4 : 4 + plan.held], refs[4 + plan.held :]
    kept, refs = refs[0], refs[1:]
    sent, refs = (refs[0], refs[1:]) if sections > 1 else (None, refs)
    cotangent, grads, left, right, share = refs
    rows, width, rank = plan.rows, streams.shape[2], hiddens.shape[2]
    block = kept.shape[1]
    replica = lax.axis_index("dp")
    step = rows // len(arrived)
    for j, ref in enumerate(arrived):
        cotangent[0, pl.ds(j * step, step), :] = ref[...]
    whole_blocks = block % 128 == 0

    def hand_out(me, s, starts):
        turn = (s + sections - me) % sections if isinstance(me, int) else lax.rem(s + sections - me, sections)
        places = [pl.ds(number * block if whole_blocks else start, block) for number, start in enumerate(starts)]

        def keep():
            for number, place in enumerate(places):
                kept[number] = share[place, :]

        def send():
            for number, place in enumerate(places):
                sent[turn - 1, number] = share[place, :].astype(jnp.bfloat16)

        if isinstance(me, int):
            keep() if turn == 0 else send()
            return
        pl.when(turn == 0)(keep)
        if sections > 1:
            pl.when(turn > 0)(send)

    def body(me, weight_of):
        for s in reversed(range(sections)):
            weight = weight_of(s)
            now, later = (sections - 1 - s) % 2, (sections - s) % 2
            scale = scales[s][:, :1]
            correction = 0.0
            for columns in chunks(rank):
                hidden = hiddens[s, :, columns].astype(jnp.float32)
                value = dot(cotangent[now], weight[:, columns], ((1,), (0,))) * (1.0 - hidden * hidden)
                grad = value.astype(jnp.bfloat16)
                grads[:, columns] = grad
                right[:rows, columns] = (value * scale).astype(jnp.bfloat16)
                correction += lanes(grad.astype(jnp.float32) * inputs[s, :, columns])
            right[rows:, :] = hiddens[s]
            starts = [
                pl.multiple_of(jnp.bitwise_xor(replica, mask_of(number, plan.order(s)[::-1])) * block, block)
                for number in range(plan.blocks)
            ]
            if whole_blocks:
                reads = [(pl.ds(start, block), pl.ds(number * block, block)) for number, start in enumerate(starts)]
            else:
                reads = [(columns, columns) for columns in chunks(width)]
            for columns, place in reads:
                left[:rows, place] = streams[s, :, columns]
                left[rows:, place] = cotangent[now, :, columns]
            if s > 0:
                correction = jnp.sum(correction, axis=1, keepdims=True) * (1.0 / width) * scale * scale
                for columns in chunks(width):
                    value = dot(grads[...], weight[columns, :], ((1,), (1,)))
                    value = cotangent[now, :, columns].astype(jnp.float32) + scale * value
                    value = value - correction * streams[s, :, columns].astype(jnp.float32)
                    cotangent[later, :, columns] = value.astype(jnp.bfloat16)
            for columns in chunks(rank):
                share[:, columns] = dot(left[...], right[:, columns], ((0,), (0,)))
            hand_out(me, s, starts)

    by_section(plan, weights, body)


def on_device(node_table, tiles, neighbours, distances, proj, upstream):
    sections, replicas = lax.axis_size("section"), lax.axis_size("dp")
    micro_count, row_count, near = distances.shape
    nodes, width = node_table.shape
    rank = proj.shape[2]
    points = micro_count * row_count
    plan = Plan(sections, replicas, points)
    rows, unit, block = plan.rows, plan.unit, width // replicas
    me = lax.axis_index("section")

    in_vmem = pl.BlockSpec(memory_space=pltpu.VMEM)
    anywhere = pl.BlockSpec(memory_space=pl.ANY)
    bf16, f32 = jnp.bfloat16, jnp.float32
    in_hbm = functools.partial(pltpu.with_memory_space_constraint, memory_space=pltpu.HBM)
    flat_upstream = upstream.reshape(points, width)
    limit = pltpu.CompilerParams(vmem_limit_bytes=LIMIT)
    packs = [pltpu.VMEM((2 * near, points), f32)]
    if plan.relayed:
        packs += [pltpu.VMEM((points // 2, width), bf16)] * 2
    arrays = (tiles, neighbours.transpose(0, 2, 1), distances.transpose(0, 2, 1))
    prepare = pl.pallas_call(
        functools.partial(prepare_kernel, plan),
        out_shape=tuple(packs),
        in_specs=[anywhere] * 4,
        out_specs=(in_vmem,) * len(packs),
        scratch_shapes=[pltpu.VMEM(array.shape, array.dtype) for array in arrays] + [pltpu.SemaphoreType.DMA((5,))],
        compiler_params=limit,
        name="prepare",
    )
    small, *halves = prepare(*map(in_hbm, (*arrays, flat_upstream)))

    def part_of(array, axis, j):
        if plan.parts == 1:
            return array
        part = sum(jnp.where(me == section, plan.units_of(section)[j][1], 0) for section in range(sections))
        return lax.dynamic_slice_in_dim(array, part * unit, unit, axis)

    def unit_route(j):
        return lambda section, replica: (section, replica ^ plan.source_mask(section, j))

    def small_route(j):
        if plan.parts > 1 or j > 0:
            return unit_route(j)
        last = sections - 1
        return lambda section, replica: (last - section, replica ^ plan.source_mask(last - section, j))

    def relay_route(section, replica):
        return sections - 1 - section, replica ^ (1 << plan.shared[1 - section])

    weights = [in_hbm(proj)]
    for turn in range(1, sections):
        weights.append(permute(proj, plan, lambda section, replica: ((section - turn) % sections, replica)))
    if plan.relayed:
        arrived = []
        for j in range(2):
            arrived.append(permute(halves[j], plan, unit_route(0)))
        near = permute(small, plan, small_route(0))
        across = permute(near, plan, relay_route)
        arrived.append(permute(arrived[0], plan, relay_route))
        arrived.append(halves[0])
        small_units = [near, across, small]
    else:
        arrived = [permute(part_of(flat_upstream, 0, j), plan, unit_route(j)) for j in range(plan.units)]
        small_units = [permute(part_of(small, 1, j), plan, small_route(j)) for j in range(plan.units)]

    formed = plan.blocks * block if block % 128 == 0 else width
    load = pl.pallas_call(
        functools.partial(load_kernel, plan),
        out_shape=(
            pltpu.VMEM((2 * nodes, width), bf16),
            pltpu.VMEM((width, rank) if sections == 2 else (sections, width, rank), bf16),
        ),
        in_specs=[anywhere] * (1 + plan.loads),
        out_specs=(in_vmem,) * 2,
        scratch_shapes=[pltpu.SemaphoreType.DMA((2 + plan.loads,))],
        compiler_params=limit,
        name="load",
    )
    forward = pl.pallas_call(
        functools.partial(forward_kernel, plan),
        out_shape=(
            pltpu.VMEM((sections, rows, width), bf16),
            pltpu.VMEM((sections, rows, rank), bf16),
            pltpu.VMEM((sections, rows, rank), f32),
            pltpu.VMEM((sections, rows, 128), f32),
        ),
        in_specs=[in_vmem] * (len(small_units) + 1 + plan.held),
        out_specs=(in_vmem,) * 4,
        scratch_shapes=[pltpu.VMEM((rows, 128), f32)],
        cost_estimate=pl.CostEstimate(
            flops=4 * sections * rows * width * rank, bytes_accessed=6 * width * rank, transcendentals=rows * rank
        ),
        compiler_params=limit,
        name="forward",
    )
    twice, held = load(in_hbm(node_table), *weights[: plan.loads])
    held = [held, weights[1].reshape(width, rank)] if sections == 2 else [held]
    streams, hiddens, inputs, scales = forward(*small_units, twice, *held)
    shapes = [jax.ShapeDtypeStruct((plan.blocks, block, rank), f32)]
    if sections > 1:
        shapes.append(jax.ShapeDtypeStruct((sections - 1, plan.blocks, block, rank), bf16))
    outs = pl.pallas_call(
        functools.partial(backward_kernel, plan),
        out_shape=tuple(shapes),
        in_specs=[in_vmem] * (len(arrived) + 4 + plan.held),
        out_specs=(in_vmem,) * len(shapes),
        scratch_shapes=[
            pltpu.VMEM((2, rows, width), bf16),
            pltpu.VMEM((rows, rank), bf16),
            pltpu.VMEM((2 * rows, formed), bf16),
            pltpu.VMEM((2 * rows, rank), bf16),
            pltpu.VMEM((formed, rank), f32),
        ],
        cost_estimate=pl.CostEstimate(
            flops=6 * sections * rows * width * rank, bytes_accessed=6 * width * rank, transcendentals=0
        ),
        compiler_params=limit,
        name="backward",
    )(*arrived, streams, hiddens, inputs, scales, *held)
    total = outs[0]
    for turn in range(1, sections):
        total = total + permute(
            outs[1][turn - 1], plan, lambda section, replica: ((section + turn) % sections, replica)
        ).astype(f32)
    left = plan.blocks
    stage = 0
    while left > 1:
        left //= 2

        def route(section, replica):
            return section, replica ^ (1 << plan.order(section)[stage])

        total = total[:left] + permute(total[left:].astype(bf16), plan, route).astype(f32)
        stage += 1
    return total * (1.0 / math.sqrt(points * replicas))


def solution(mesh):
    return jax.shard_map(
        on_device,
        mesh=mesh,
        in_specs=(
            P(),
            P(None, "dp"),
            P(None, "dp", None),
            P(None, "dp", None),
            P("section", None, None),
            P(None, "dp", None),
        ),
        out_specs=P("section", "dp", None),
        check_vma=False,
    )
```

profile of v0, /device:TPU:0, one launch (start us, length us, event | category | flops | bytes accessed | tf_op | source)
XLA Modules:
  0.0 40.7 jit_solution(18287378665690541921)
XLA Ops:
  0.0 0.5 %collective-permute-start.5 = (bf16[1,2048,512]{2,1,0:T(8,128)(2,1)}, bf16[1,2048,512]{2,1,0:T(8,128)(2,1)S(1)}, u32[]{:S(2)}, u32[]{:S(2)}) collective-permute-start(bf16[1,2048,512]{2,1,0:T(8,128)(2,1)} %refs_0_.3), channel_id=1, source_target_pairs={{0,16},{1,17},{2,18},{3,19},{4,20},{5,21},{6,22},{7,23},{8,24},{9,... | collective-permute-start | bytes 6291464 | tf_op jit(solution)/shard_map/ppermute | solution.py:57
  0.5 1.1 %prepare.1 = (f32[16,128]{1,0:T(8,128)S(1)}, bf16[64,2048]{1,0:T(8,128)(2,1)S(1)}, bf16[64,2048]{1,0:T(8,128)(2,1)S(1)}) custom-call(s32[4,32]{1,0:T(4,128)} %refs_0_.2, s32[4,8,32]{2,1,0:T(8,128)} %bitcast.9, f32[4,8,32]{2,1,0:T(8,128)} %bitcast.10, bf16[128,2048]{1,0:T(8,128)(2,1)} %bitcast.8), custom_call_target="tpu_custom_call" | custom-call | tf_op jit(solution)/shard_map/prepare/pallas_call | solution.py:293
  1.6 2.6 %collective-permute-start = (bf16[64,2048]{1,0:T(8,128)(2,1)S(1)}, bf16[64,2048]{1,0:T(8,128)(2,1)S(1)}, u32[]{:S(2)}, u32[]{:S(2)}) collective-permute-start(bf16[64,2048]{1,0:T(8,128)(2,1)S(1)} %get-tuple-element.16.refs_3_), channel_id=1, source_target_pairs={{0,4},{1,5},{2,6},{3,7},{4,0},{5,1},{6,2},{7,3},{8,12},{9,13},{10,... | collective-permute-start | bytes 786440 | tf_op jit(solution)/shard_map/ppermute | solution.py:57
  4.3 0.1 collective-permute-start.1
  4.3 4.3 %collective-permute-done.refs_0_ = bf16[64,2048]{1,0:T(8,128)(2,1)S(1)} collective-permute-done((bf16[64,2048]{1,0:T(8,128)(2,1)S(1)}, bf16[64,2048]{1,0:T(8,128)(2,1)S(1)}, u32[]{:S(2)}, u32[]{:S(2)}) %collective-permute-start) | collective-permute-done | bytes 262176 | tf_op jit(solution)/shard_map/ppermute | solution.py:57
  8.6 1.2 %collective-permute-start.2 = (bf16[64,2048]{1,0:T(8,128)(2,1)S(1)}, bf16[64,2048]{1,0:T(8,128)(2,1)S(1)}, u32[]{:S(2)}, u32[]{:S(2)}) collective-permute-start(bf16[64,2048]{1,0:T(8,128)(2,1)S(1)} %collective-permute-done.refs_0_), channel_id=1, source_target_pairs={{0,17},{1,16},{2,19},{3,18},{4,21},{5,20},{6,23},{7,22},{8,25},{9,... | collective-permute-start | bytes 786440 | tf_op jit(solution)/shard_map/ppermute | solution.py:57
  9.8 2.0 %collective-permute-start.3 = (f32[16,128]{1,0:T(8,128)S(1)}, f32[16,128]{1,0:T(8,128)S(1)}, u32[]{:S(2)}, u32[]{:S(2)}) collective-permute-start(f32[16,128]{1,0:T(8,128)S(1)} %get-tuple-element.18.refs_2_), channel_id=1, source_target_pairs={{0,17},{1,16},{2,19},{3,18},{4,21},{5,20},{6,23},{7,22},{8,25},{9,... | collective-permute-start | bytes 24584 | tf_op jit(solution)/shard_map/ppermute | solution.py:57
  11.8 2.7 %collective-permute-done.3.refs_0_ = f32[16,128]{1,0:T(8,128)S(1)} collective-permute-done((f32[16,128]{1,0:T(8,128)S(1)}, f32[16,128]{1,0:T(8,128)S(1)}, u32[]{:S(2)}, u32[]{:S(2)}) %collective-permute-start.3) | collective-permute-done | bytes 8224 | tf_op jit(solution)/shard_map/ppermute | solution.py:57
  14.5 1.5 %collective-permute-start.4 = (f32[16,128]{1,0:T(8,128)S(1)}, f32[16,128]{1,0:T(8,128)S(1)}, u32[]{:S(2)}, u32[]{:S(2)}) collective-permute-start(f32[16,128]{1,0:T(8,128)S(1)} %collective-permute-done.3.refs_0_), channel_id=1, source_target_pairs={{0,17},{1,16},{2,19},{3,18},{4,21},{5,20},{6,23},{7,22},{8,25},{9,... | collective-permute-start | bytes 24584 | tf_op jit(solution)/shard_map/ppermute | solution.py:57
  16.0 1.9 %load.1 = (bf16[256,2048]{1,0:T(8,128)(2,1)S(1)}, bf16[2048,512]{1,0:T(8,128)(2,1)S(1)}) custom-call(bf16[128,2048]{1,0:T(8,128)(2,1)} %table.1, bf16[1,2048,512]{2,1,0:T(8,128)(2,1)} %refs_0_.3), custom_call_target="tpu_custom_call" | custom-call | tf_op jit(solution)/shard_map/load/pallas_call | solution.py:359
  17.9 0.0 collective-permute-done.4.refs_1_
  17.9 0.0 collective-permute-done.5
  18.0 2.6 %forward.1 = (bf16[2,256,2048]{2,1,0:T(8,128)(2,1)S(1)}, bf16[2,256,512]{2,1,0:T(8,128)(2,1)S(1)}, f32[2,256,512]{2,1,0:T(8,128)S(1)}, f32[2,256,128]{2,1,0:T(8,128)S(1)}) custom-call(f32[16,128]{1,0:T(8,128)S(1)} %collective-permute-done.3.refs_0_, f32[16,128]{1,0:T(8,128)S(1)} %collective-permute-done.4.refs_1_, f32[16,128]{1,0:T(8,128)S(1)} %get-tuple-element.18.refs_2_, ...), custom_call_target="tpu_custom_call" | custom-call | flops 2147483648 | bytes 6291456 | tf_op jit(solution)/shard_map/forward/pallas_call | solution.py:361
  20.6 0.0 collective-permute-done.1.refs_1_
  20.6 0.0 collective-permute-done.2.refs_2_
  20.6 3.0 %backward.1 = (f32[4,128,512]{2,1,0:T(8,128)S(1)}, bf16[1,4,128,512]{3,2,1,0:T(8,128)(2,1)S(1)}) custom-call(bf16[64,2048]{1,0:T(8,128)(2,1)S(1)} %collective-permute-done.refs_0_, bf16[64,2048]{1,0:T(8,128)(2,1)S(1)} %collective-permute-done.1.refs_1_, bf16[64,2048]{1,0:T(8,128)(2,1)S(1)} %collective-permute-done.2.refs_2_, ...), custom_call_target="tpu_custom_call" | custom-call | flops 3221225472 | bytes 6291456 | tf_op jit(solution)/shard_map/backward/pallas_call | solution.py:365
  23.6 0.7 %collective-permute-start.6 = (bf16[4,128,512]{2,1,0:T(8,128)(2,1)S(1)}, bf16[4,128,512]{2,1,0:T(8,128)(2,1)S(1)}, u32[]{:S(2)}, u32[]{:S(2)}) collective-permute-start(bf16[4,128,512]{2,1,0:T(8,128)(2,1)S(1)} %bitcast.7), channel_id=1, source_target_pairs={{0,16},{1,17},{2,18},{3,19},{4,20},{5,21},{6,22},{7,23},{8,24},{9,... | collective-permute-start | bytes 1572872 | tf_op jit(solution)/shard_map/ppermute | solution.py:57
  24.3 1.5 %collective-permute-done.6 = bf16[4,128,512]{2,1,0:T(8,128)(2,1)S(1)} collective-permute-done((bf16[4,128,512]{2,1,0:T(8,128)(2,1)S(1)}, bf16[4,128,512]{2,1,0:T(8,128)(2,1)S(1)}, u32[]{:S(2)}, u32[]{:S(2)}) %collective-permute-start.6) | collective-permute-done | bytes 524320 | tf_op jit(solution)/shard_map/ppermute | solution.py:57
  25.9 0.2 convert_add_fusion
  26.1 1.6 %collective-permute-start.7 = (bf16[2,128,512]{2,1,0:T(8,128)(2,1)S(1)}, bf16[2,128,512]{2,1,0:T(8,128)(2,1)S(1)}, u32[]{:S(2)}, u32[]{:S(2)}) collective-permute-start(bf16[2,128,512]{2,1,0:T(8,128)(2,1)S(1)} %slice.28), channel_id=1, source_target_pairs={{0,2},{1,3},{2,0},{3,1},{4,6},{5,7},{6,4},{7,5},{8,10},{9,11},{10,... | collective-permute-start | bytes 786440 | tf_op jit(solution)/shard_map/ppermute | solution.py:57
  27.7 4.9 %collective-permute-done.7 = bf16[2,128,512]{2,1,0:T(8,128)(2,1)S(1)} collective-permute-done((bf16[2,128,512]{2,1,0:T(8,128)(2,1)S(1)}, bf16[2,128,512]{2,1,0:T(8,128)(2,1)S(1)}, u32[]{:S(2)}, u32[]{:S(2)}) %collective-permute-start.7) | collective-permute-done | bytes 262176 | tf_op jit(solution)/shard_map/ppermute | solution.py:57
  32.6 0.1 slice_add_fusion
  32.7 2.7 %collective-permute-start.8 = (bf16[1,128,512]{2,1,0:T(8,128)(2,1)S(1)}, bf16[1,128,512]{2,1,0:T(8,128)(2,1)S(1)}, u32[]{:S(2)}, u32[]{:S(2)}) collective-permute-start(bf16[1,128,512]{2,1,0:T(8,128)(2,1)S(1)} %slice.29), channel_id=1, source_target_pairs={{0,8},{1,9},{2,10},{3,11},{4,12},{5,13},{6,14},{7,15},{8,0},{9,1},... | collective-permute-start | bytes 393224 | tf_op jit(solution)/shard_map/ppermute | solution.py:57
  35.3 4.7 %collective-permute-done.8 = bf16[1,128,512]{2,1,0:T(8,128)(2,1)S(1)} collective-permute-done((bf16[1,128,512]{2,1,0:T(8,128)(2,1)S(1)}, bf16[1,128,512]{2,1,0:T(8,128)(2,1)S(1)}, u32[]{:S(2)}, u32[]{:S(2)}) %collective-permute-start.8) | collective-permute-done | bytes 131104 | tf_op jit(solution)/shard_map/ppermute | solution.py:57
  40.0 0.7 %fusion = f32[1,128,512]{2,1,0:T(8,128)} fusion(f32[2,128,512]{2,1,0:T(8,128)S(1)} %slice_add_fusion, bf16[1,128,512]{2,1,0:T(8,128)(2,1)S(1)} %collective-permute-done.8), kind=kLoop, calls=%fused_computation.5 | loop fusion | flops 196608 | bytes 655360 | tf_op jit(solution)/shard_map/mul | solution.py:398
  (2 shorter events, 0.1 us)
Async XLA Ops:
  0.0 17.9 %collective-permute-start.5 = (bf16[1,2048,512]{2,1,0:T(8,128)(2,1)}, bf16[1,2048,512]{2,1,0:T(8,128)(2,1)S(1)}, u32[]{:S(2)}, u32[]{:S(2)}) collective-permute-start(bf16[1,2048,512]{2,1,0:T(8,128)(2,1)} %refs_0_.3), channel_id=1, source_target_pairs={{0,16},{1,17},{2,18},{3,19},{4,20},{5,21},{6,22},{7,23},{8,24},{9,... | collective-permute-start | bytes 6291464 | tf_op jit(solution)/shard_map/ppermute | solution.py:57
  1.6 7.0 %collective-permute-start = (bf16[64,2048]{1,0:T(8,128)(2,1)S(1)}, bf16[64,2048]{1,0:T(8,128)(2,1)S(1)}, u32[]{:S(2)}, u32[]{:S(2)}) collective-permute-start(bf16[64,2048]{1,0:T(8,128)(2,1)S(1)} %get-tuple-element.16.refs_3_), channel_id=1, source_target_pairs={{0,4},{1,5},{2,6},{3,7},{4,0},{5,1},{6,2},{7,3},{8,12},{9,13},{10,... | collective-permute-start | bytes 786440 | tf_op jit(solution)/shard_map/ppermute | solution.py:57
  4.3 16.4 %collective-permute-start.1 = (bf16[64,2048]{1,0:T(8,128)(2,1)S(1)}, bf16[64,2048]{1,0:T(8,128)(2,1)S(1)}, u32[]{:S(2)}, u32[]{:S(2)}) collective-permute-start(bf16[64,2048]{1,0:T(8,128)(2,1)S(1)} %get-tuple-element.17), channel_id=1, source_target_pairs={{0,4},{1,5},{2,6},{3,7},{4,0},{5,1},{6,2},{7,3},{8,12},{9,13},{10,... | collective-permute-start | bytes 786440 | tf_op jit(solution)/shard_map/ppermute | solution.py:57
  8.6 12.0 %collective-permute-start.2 = (bf16[64,2048]{1,0:T(8,128)(2,1)S(1)}, bf16[64,2048]{1,0:T(8,128)(2,1)S(1)}, u32[]{:S(2)}, u32[]{:S(2)}) collective-permute-start(bf16[64,2048]{1,0:T(8,128)(2,1)S(1)} %collective-permute-done.refs_0_), channel_id=1, source_target_pairs={{0,17},{1,16},{2,19},{3,18},{4,21},{5,20},{6,23},{7,22},{8,25},{9,... | collective-permute-start | bytes 786440 | tf_op jit(solution)/shard_map/ppermute | solution.py:57
  9.8 4.7 %collective-permute-start.3 = (f32[16,128]{1,0:T(8,128)S(1)}, f32[16,128]{1,0:T(8,128)S(1)}, u32[]{:S(2)}, u32[]{:S(2)}) collective-permute-start(f32[16,128]{1,0:T(8,128)S(1)} %get-tuple-element.18.refs_2_), channel_id=1, source_target_pairs={{0,17},{1,16},{2,19},{3,18},{4,21},{5,20},{6,23},{7,22},{8,25},{9,... | collective-permute-start | bytes 24584 | tf_op jit(solution)/shard_map/ppermute | solution.py:57
  14.5 3.4 %collective-permute-start.4 = (f32[16,128]{1,0:T(8,128)S(1)}, f32[16,128]{1,0:T(8,128)S(1)}, u32[]{:S(2)}, u32[]{:S(2)}) collective-permute-start(f32[16,128]{1,0:T(8,128)S(1)} %collective-permute-done.3.refs_0_), channel_id=1, source_target_pairs={{0,17},{1,16},{2,19},{3,18},{4,21},{5,20},{6,23},{7,22},{8,25},{9,... | collective-permute-start | bytes 24584 | tf_op jit(solution)/shard_map/ppermute | solution.py:57
  23.6 2.2 %collective-permute-start.6 = (bf16[4,128,512]{2,1,0:T(8,128)(2,1)S(1)}, bf16[4,128,512]{2,1,0:T(8,128)(2,1)S(1)}, u32[]{:S(2)}, u32[]{:S(2)}) collective-permute-start(bf16[4,128,512]{2,1,0:T(8,128)(2,1)S(1)} %bitcast.7), channel_id=1, source_target_pairs={{0,16},{1,17},{2,18},{3,19},{4,20},{5,21},{6,22},{7,23},{8,24},{9,... | collective-permute-start | bytes 1572872 | tf_op jit(solution)/shard_map/ppermute | solution.py:57
  26.1 6.4 %collective-permute-start.7 = (bf16[2,128,512]{2,1,0:T(8,128)(2,1)S(1)}, bf16[2,128,512]{2,1,0:T(8,128)(2,1)S(1)}, u32[]{:S(2)}, u32[]{:S(2)}) collective-permute-start(bf16[2,128,512]{2,1,0:T(8,128)(2,1)S(1)} %slice.28), channel_id=1, source_target_pairs={{0,2},{1,3},{2,0},{3,1},{4,6},{5,7},{6,4},{7,5},{8,10},{9,11},{10,... | collective-permute-start | bytes 786440 | tf_op jit(solution)/shard_map/ppermute | solution.py:57
  32.7 7.3 %collective-permute-start.8 = (bf16[1,128,512]{2,1,0:T(8,128)(2,1)S(1)}, bf16[1,128,512]{2,1,0:T(8,128)(2,1)S(1)}, u32[]{:S(2)}, u32[]{:S(2)}) collective-permute-start(bf16[1,128,512]{2,1,0:T(8,128)(2,1)S(1)} %slice.29), channel_id=1, source_target_pairs={{0,8},{1,9},{2,10},{3,11},{4,12},{5,13},{6,14},{7,15},{8,0},{9,1},... | collective-permute-start | bytes 393224 | tf_op jit(solution)/shard_map/ppermute | solution.py:57
where the time goes:
time: 40.9 us; the launch traced here: 40.7 us
  waiting for transfers between devices  18 us (44%)
  starting transfers between devices  12.8 us (31%)
  Pallas kernels  8.73 us (21%)
  other arithmetic  1 us (2%)
    ppermute x9, waiting for transfers between devices, permute(): return lax.ppermute(block, AXES, pairs)  18 us
    ppermute x9, starting transfers between devices, permute(): return lax.ppermute(block, AXES, pairs)  12.8 us
    pallas_call x1, Pallas kernels, on_device(): pl.pallas_call(functools.partial(backward_kernel, plan), out_shape=tuple(...  3.01 us
    pallas_call x1, Pallas kernels, on_device(): streams, hiddens, inputs, scales = forward(*small_units, twice, *held)  2.64 us
    pallas_call x1, Pallas kernels, on_device(): twice, held = load(in_hbm(node_table), *weights[:plan.loads])  1.95 us
    pallas_call x1, Pallas kernels, on_device(): small, *halves = prepare(*map(in_hbm, (*arrays, flat_upstream)))  1.12 us
  transfers between devices with their start and end apart: 9, of which 5 were waited for; matrix products, arithmetic and copies ran while one was open for 0% of the time, Pallas kernels for 14%

commit v1 on v0

--- a/solution.py
+++ b/solution.py
@@ -12,7 +12,7 @@
 
 epsilon = 1e-05
 AXES = ("section", "dp")
-SHARED_BITS = (2, 0)
+SHARED_BITS = (0, 2)
 LIMIT = 36 << 20
 
 
@@ -108,16 +108,15 @@
 
 def load_kernel(plan, table, *refs):
     weights, refs = refs[: plan.loads], refs[plan.loads :]
-    twice, held, sem = refs
-    nodes = table.shape[0]
-    copies = [pltpu.make_async_copy(table, twice.at[pl.ds(i * nodes, nodes)], sem.at[i]) for i in range(2)]
+    table_held, held, sem = refs
+    copies = [pltpu.make_async_copy(table, table_held, sem.at[0])]
     if plan.sections == 2:
-        copies.append(pltpu.make_async_copy(weights[0].at[0], held, sem.at[2]))
+        copies.append(pltpu.make_async_copy(weights[0].at[0], held, sem.at[1]))
     else:
         me = lax.axis_index("section")
         for turn, weight in enumerate(weights):
             place = lax.rem(me + turn, plan.sections)
-            copies.append(pltpu.make_async_copy(weight.at[0], held.at[place], sem.at[2 + turn]))
+            copies.append(pltpu.make_async_copy(weight.at[0], held.at[place], sem.at[1 + turn]))
     for copy in copies:
         copy.start()
     for copy in copies:
@@ -127,10 +126,12 @@
 def forward_kernel(plan, *refs):
     units, sections = plan.units, plan.sections
     given = 3 if plan.relayed else units
-    small, twice, refs = refs[:given], refs[given], refs[given + 1 :]
+    small, table, refs = refs[:given], refs[given], refs[given + 1 :]
     weights, refs = refs[: plan.held], refs[plan.held :]
-    streams, hiddens, inputs, scales, total = refs
-    nodes, width = twice.shape[0] // 2, twice.shape[1]
+    streams, hiddens, inputs, scales, twice, total = refs
+    nodes, width = table.shape
+    twice[:nodes, :] = table[...]
+    twice[nodes:, :] = table[...]
     rank = hiddens.shape[2]
     me = lax.axis_index("section")
     count = small[0].shape[0] // 2
@@ -140,7 +141,7 @@
         near, across, own = packed
         low_half = lax.broadcasted_iota(jnp.int32, own.shape, 1) < half
         mixed = jnp.where(low_half == (me == 0), own, across)
-        packed = [jnp.where(me == 0, a, b) for a, b in ((near, pltpu.roll(near, half, 1)), (pltpu.roll(mixed, half, 1), mixed))]
+        packed = [jnp.where(me == 0, array, pltpu.roll(array, half, 1)) for array in (near, mixed)]
     selectors = []
     for j in range(units):
         index = packed[j][:count, :].astype(jnp.int32)
@@ -186,16 +187,20 @@
     by_section(plan, weights, body)
 
 
-def backward_kernel(plan, *refs):
+def backward_kernel(plan, given, low, rows, *refs):
     sections = plan.sections
-    given = 4 if plan.relayed else plan.units
     arrived, refs = refs[:given], refs[given:]
     streams, hiddens, inputs, scales = refs[:4]
     weights, refs = refs[4 : 4 + plan.held], refs[4 + plan.held :]
+    formed = ()
+    if low > 0:
+        outs = min(sections, 2)
+        formed, refs = refs[:outs], refs[outs:]
+    span = pl.ds(low, rows)
     kept, refs = refs[0], refs[1:]
     sent, refs = (refs[0], refs[1:]) if sections > 1 else (None, refs)
     cotangent, grads, left, right, share = refs
-    rows, width, rank = plan.rows, streams.shape[2], hiddens.shape[2]
+    width, rank = streams.shape[2], hiddens.shape[2]
     block = kept.shape[1]
     replica = lax.axis_index("dp")
     step = rows // len(arrived)
@@ -209,11 +214,14 @@
 
         def keep():
             for number, place in enumerate(places):
-                kept[number] = share[place, :]
+                value = share[place, :]
+                kept[number] = value + formed[0][number] if formed else value
 
         def send():
             for number, place in enumerate(places):
-                sent[turn - 1, number] = share[place, :].astype(jnp.bfloat16)
+                value = share[place, :]
+                value = value + formed[1][turn - 1, number] if formed else value
+                sent[turn - 1, number] = value.astype(sent.dtype)
 
         if isinstance(me, int):
             keep() if turn == 0 else send()
@@ -226,16 +234,16 @@
         for s in reversed(range(sections)):
             weight = weight_of(s)
             now, later = (sections - 1 - s) % 2, (sections - s) % 2
-            scale = scales[s][:, :1]
+            scale = scales[s, span, :][:, :1]
             correction = 0.0
             for columns in chunks(rank):
-                hidden = hiddens[s, :, columns].astype(jnp.float32)
+                hidden = hiddens[s, span, columns].astype(jnp.float32)
                 value = dot(cotangent[now], weight[:, columns], ((1,), (0,))) * (1.0 - hidden * hidden)
                 grad = value.astype(jnp.bfloat16)
                 grads[:, columns] = grad
                 right[:rows, columns] = (value * scale).astype(jnp.bfloat16)
-                correction += lanes(grad.astype(jnp.float32) * inputs[s, :, columns])
-            right[rows:, :] = hiddens[s]
+                correction += lanes(grad.astype(jnp.float32) * inputs[s, span, columns])
+            right[rows:, :] = hiddens[s, span, :]
             starts = [
                 pl.multiple_of(jnp.bitwise_xor(replica, mask_of(number, plan.order(s)[::-1])) * block, block)
                 for number in range(plan.blocks)
@@ -245,14 +253,14 @@
             else:
                 reads = [(columns, columns) for columns in chunks(width)]
             for columns, place in reads:
-                left[:rows, place] = streams[s, :, columns]
+                left[:rows, place] = streams[s, span, columns]
                 left[rows:, place] = cotangent[now, :, columns]
             if s > 0:
                 correction = jnp.sum(correction, axis=1, keepdims=True) * (1.0 / width) * scale * scale
                 for columns in chunks(width):
                     value = dot(grads[...], weight[columns, :], ((1,), (1,)))
                     value = cotangent[now, :, columns].astype(jnp.float32) + scale * value
-                    value = value - correction * streams[s, :, columns].astype(jnp.float32)
+                    value = value - correction * streams[s, span, columns].astype(jnp.float32)
                     cotangent[later, :, columns] = value.astype(jnp.bfloat16)
             for columns in chunks(rank):
                 share[:, columns] = dot(left[...], right[:, columns], ((0,), (0,)))
@@ -320,7 +328,7 @@
         near = permute(small, plan, small_route(0))
         across = permute(near, plan, relay_route)
         arrived.append(permute(arrived[0], plan, relay_route))
-        arrived.append(halves[0])
+        arrived.insert(2, halves[0])
         small_units = [near, across, small]
     else:
         arrived = [permute(part_of(flat_upstream, 0, j), plan, unit_route(j)) for j in range(plan.units)]
@@ -330,12 +338,12 @@
     load = pl.pallas_call(
         functools.partial(load_kernel, plan),
         out_shape=(
-            pltpu.VMEM((2 * nodes, width), bf16),
+            pltpu.VMEM((nodes, width), bf16),
             pltpu.VMEM((width, rank) if sections == 2 else (sections, width, rank), bf16),
         ),
         in_specs=[anywhere] * (1 + plan.loads),
         out_specs=(in_vmem,) * 2,
-        scratch_shapes=[pltpu.SemaphoreType.DMA((2 + plan.loads,))],
+        scratch_shapes=[pltpu.SemaphoreType.DMA((1 + plan.loads,))],
         compiler_params=limit,
         name="load",
     )
@@ -349,37 +357,41 @@
         ),
         in_specs=[in_vmem] * (len(small_units) + 1 + plan.held),
         out_specs=(in_vmem,) * 4,
-        scratch_shapes=[pltpu.VMEM((rows, 128), f32)],
+        scratch_shapes=[pltpu.VMEM((2 * nodes, width), bf16), pltpu.VMEM((rows, 128), f32)],
         cost_estimate=pl.CostEstimate(
             flops=4 * sections * rows * width * rank, bytes_accessed=6 * width * rank, transcendentals=rows * rank
         ),
         compiler_params=limit,
         name="forward",
     )
-    twice, held = load(in_hbm(node_table), *weights[: plan.loads])
+    table, held = load(in_hbm(node_table), *weights[: plan.loads])
     held = [held, weights[1].reshape(width, rank)] if sections == 2 else [held]
-    streams, hiddens, inputs, scales = forward(*small_units, twice, *held)
-    shapes = [jax.ShapeDtypeStruct((plan.blocks, block, rank), f32)]
-    if sections > 1:
-        shapes.append(jax.ShapeDtypeStruct((sections - 1, plan.blocks, block, rank), bf16))
-    outs = pl.pallas_call(
-        functools.partial(backward_kernel, plan),
-        out_shape=tuple(shapes),
-        in_specs=[in_vmem] * (len(arrived) + 4 + plan.held),
-        out_specs=(in_vmem,) * len(shapes),
-        scratch_shapes=[
-            pltpu.VMEM((2, rows, width), bf16),
-            pltpu.VMEM((rows, rank), bf16),
-            pltpu.VMEM((2 * rows, formed), bf16),
-            pltpu.VMEM((2 * rows, rank), bf16),
-            pltpu.VMEM((formed, rank), f32),
-        ],
-        cost_estimate=pl.CostEstimate(
-            flops=6 * sections * rows * width * rank, bytes_accessed=6 * width * rank, transcendentals=0
-        ),
-        compiler_params=limit,
-        name="backward",
-    )(*arrived, streams, hiddens, inputs, scales, *held)
+    streams, hiddens, inputs, scales = forward(*small_units, table, *held)
+    cuts = [(arrived, 0, rows)]
+    outs = ()
+    for given, low, count in cuts:
+        last = low + count == rows
+        shapes = [pltpu.VMEM((plan.blocks, block, rank), f32)]
+        if sections > 1:
+            shapes.append(pltpu.VMEM((sections - 1, plan.blocks, block, rank), bf16 if last else f32))
+        backward = pl.pallas_call(
+            functools.partial(backward_kernel, plan, len(given), low, count),
+            out_shape=tuple(shapes),
+            in_specs=[in_vmem] * (len(given) + 4 + plan.held + len(outs)),
+            out_specs=(in_vmem,) * len(shapes),
+            scratch_shapes=[
+                pltpu.VMEM((2, count, width), bf16),
+                pltpu.VMEM((count, rank), bf16),
+                pltpu.VMEM((2 * count, formed), bf16),
+                pltpu.VMEM((2 * count, rank), bf16),
+                pltpu.VMEM((formed, rank), f32),
+            ],
+            cost_estimate=pl.CostEstimate(
+                flops=6 * sections * count * width * rank, bytes_accessed=6 * width * rank, transcendentals=0
+            ),
+            compiler_params=limit,
+        )
+        outs = backward(*given, streams, hiddens, inputs, scales, *held, *outs)
     total = outs[0]
     for turn in range(1, sections):
         total = total + permute(

time: 40.9 us -> 40.6 us (level)
  no operation moved by 1% of the time
where the time goes in v1:
time: 40.6 us; the launch traced here: 40.5 us
  waiting for transfers between devices  17.8 us (44%)
  starting transfers between devices  12.9 us (32%)
  Pallas kernels  8.53 us (21%)
  other arithmetic  1 us (2%)
    ppermute x9, waiting for transfers between devices, permute(): return lax.ppermute(block, AXES, pairs)  17.8 us
    ppermute x9, starting transfers between devices, permute(): return lax.ppermute(block, AXES, pairs)  12.9 us
    pallas_call x1, Pallas kernels, on_device(): outs = backward(*given, streams, hiddens, inputs, scales, *held, *outs)  2.99 us
    pallas_call x1, Pallas kernels, on_device(): streams, hiddens, inputs, scales = forward(*small_units, table, *held)  2.63 us
    pallas_call x1, Pallas kernels, on_device(): table, held = load(in_hbm(node_table), *weights[:plan.loads])  1.78 us
    pallas_call x1, Pallas kernels, on_device(): small, *halves = prepare(*map(in_hbm, (*arrays, flat_upstream)))  1.12 us
  transfers between devices with their start and end apart: 9, of which 5 were waited for; matrix products, arithmetic and copies ran while one was open for 0% of the time, Pallas kernels for 14%

profile of v1, /device:TPU:0, one launch (start us, length us, event | category | flops | bytes accessed | tf_op | source)
XLA Modules:
  0.0 40.5 jit_solution(17524537698665508413)
XLA Ops:
  0.0 0.5 %collective-permute-start.5 = (bf16[1,2048,512]{2,1,0:T(8,128)(2,1)}, bf16[1,2048,512]{2,1,0:T(8,128)(2,1)S(1)}, u32[]{:S(2)}, u32[]{:S(2)}) collective-permute-start(bf16[1,2048,512]{2,1,0:T(8,128)(2,1)} %refs_0_.3), channel_id=1, source_target_pairs={{0,16},{1,17},{2,18},{3,19},{4,20},{5,21},{6,22},{7,23},{8,24},{9,... | collective-permute-start | bytes 6291464 | tf_op jit(solution)/shard_map/ppermute | solution.py:57
  0.5 1.1 %prepare.1 = (f32[16,128]{1,0:T(8,128)S(1)}, bf16[64,2048]{1,0:T(8,128)(2,1)S(1)}, bf16[64,2048]{1,0:T(8,128)(2,1)S(1)}) custom-call(s32[4,32]{1,0:T(4,128)} %refs_0_.2, s32[4,8,32]{2,1,0:T(8,128)} %bitcast.9, f32[4,8,32]{2,1,0:T(8,128)} %bitcast.10, bf16[128,2048]{1,0:T(8,128)(2,1)} %bitcast.8), custom_call_target="tpu_custom_call" | custom-call | tf_op jit(solution)/shard_map/prepare/pallas_call | solution.py:301
  1.6 2.5 %collective-permute-start = (bf16[64,2048]{1,0:T(8,128)(2,1)S(1)}, bf16[64,2048]{1,0:T(8,128)(2,1)S(1)}, u32[]{:S(2)}, u32[]{:S(2)}) collective-permute-start(bf16[64,2048]{1,0:T(8,128)(2,1)S(1)} %get-tuple-element.16.refs_2_), channel_id=1, source_target_pairs={{0,1},{1,0},{2,3},{3,2},{4,5},{5,4},{6,7},{7,6},{8,9},{9,8},{10,11... | collective-permute-start | bytes 786440 | tf_op jit(solution)/shard_map/ppermute | solution.py:57
  4.2 0.1 collective-permute-start.1
  4.2 4.3 %collective-permute-done.refs_0_ = bf16[64,2048]{1,0:T(8,128)(2,1)S(1)} collective-permute-done((bf16[64,2048]{1,0:T(8,128)(2,1)S(1)}, bf16[64,2048]{1,0:T(8,128)(2,1)S(1)}, u32[]{:S(2)}, u32[]{:S(2)}) %collective-permute-start) | collective-permute-done | bytes 262176 | tf_op jit(solution)/shard_map/ppermute | solution.py:57
  8.5 1.4 %collective-permute-start.2 = (bf16[64,2048]{1,0:T(8,128)(2,1)S(1)}, bf16[64,2048]{1,0:T(8,128)(2,1)S(1)}, u32[]{:S(2)}, u32[]{:S(2)}) collective-permute-start(bf16[64,2048]{1,0:T(8,128)(2,1)S(1)} %collective-permute-done.refs_0_), channel_id=1, source_target_pairs={{0,20},{1,21},{2,22},{3,23},{4,16},{5,17},{6,18},{7,19},{8,28},{9,... | collective-permute-start | bytes 786440 | tf_op jit(solution)/shard_map/ppermute | solution.py:57
  9.9 2.0 %collective-permute-start.3 = (f32[16,128]{1,0:T(8,128)S(1)}, f32[16,128]{1,0:T(8,128)S(1)}, u32[]{:S(2)}, u32[]{:S(2)}) collective-permute-start(f32[16,128]{1,0:T(8,128)S(1)} %get-tuple-element.18.refs_2_), channel_id=1, source_target_pairs={{0,20},{1,21},{2,22},{3,23},{4,16},{5,17},{6,18},{7,19},{8,28},{9,... | collective-permute-start | bytes 24584 | tf_op jit(solution)/shard_map/ppermute | solution.py:57
  11.8 2.6 %collective-permute-done.3.refs_0_ = f32[16,128]{1,0:T(8,128)S(1)} collective-permute-done((f32[16,128]{1,0:T(8,128)S(1)}, f32[16,128]{1,0:T(8,128)S(1)}, u32[]{:S(2)}, u32[]{:S(2)}) %collective-permute-start.3) | collective-permute-done | bytes 8224 | tf_op jit(solution)/shard_map/ppermute | solution.py:57
  14.4 1.7 %collective-permute-start.4 = (f32[16,128]{1,0:T(8,128)S(1)}, f32[16,128]{1,0:T(8,128)S(1)}, u32[]{:S(2)}, u32[]{:S(2)}) collective-permute-start(f32[16,128]{1,0:T(8,128)S(1)} %collective-permute-done.3.refs_0_), channel_id=1, source_target_pairs={{0,20},{1,21},{2,22},{3,23},{4,16},{5,17},{6,18},{7,19},{8,28},{9,... | collective-permute-start | bytes 24584 | tf_op jit(solution)/shard_map/ppermute | solution.py:57
  16.1 1.8 %load.1 = (bf16[128,2048]{1,0:T(8,128)(2,1)S(1)}, bf16[2048,512]{1,0:T(8,128)(2,1)S(1)}) custom-call(bf16[128,2048]{1,0:T(8,128)(2,1)} %table.1, bf16[1,2048,512]{2,1,0:T(8,128)(2,1)} %refs_0_.3), custom_call_target="tpu_custom_call" | custom-call | tf_op jit(solution)/shard_map/load/pallas_call | solution.py:367
  17.9 0.0 collective-permute-done.4.refs_1_
  17.9 0.0 collective-permute-done.5
  17.9 2.6 %forward.1 = (bf16[2,256,2048]{2,1,0:T(8,128)(2,1)S(1)}, bf16[2,256,512]{2,1,0:T(8,128)(2,1)S(1)}, f32[2,256,512]{2,1,0:T(8,128)S(1)}, f32[2,256,128]{2,1,0:T(8,128)S(1)}) custom-call(f32[16,128]{1,0:T(8,128)S(1)} %collective-permute-done.3.refs_0_, f32[16,128]{1,0:T(8,128)S(1)} %collective-permute-done.4.refs_1_, f32[16,128]{1,0:T(8,128)S(1)} %get-tuple-element.18.refs_2_, ...), custom_call_target="tpu_custom_call" | custom-call | flops 2147483648 | bytes 6291456 | tf_op jit(solution)/shard_map/forward/pallas_call | solution.py:369
  20.5 0.0 collective-permute-done.1.refs_1_
  20.5 0.0 collective-permute-done.2.refs_3_
  20.5 3.0 %shard_map.64 = (f32[4,128,512]{2,1,0:T(8,128)S(1)}, bf16[1,4,128,512]{3,2,1,0:T(8,128)(2,1)S(1)}) custom-call(bf16[64,2048]{1,0:T(8,128)(2,1)S(1)} %collective-permute-done.refs_0_, bf16[64,2048]{1,0:T(8,128)(2,1)S(1)} %collective-permute-done.1.refs_1_, bf16[64,2048]{1,0:T(8,128)(2,1)S(1)} %get-tuple-element.16.refs_2_, ...), custom_call_target="tpu_custom_call" | custom-call | flops 3221225472 | bytes 6291456 | tf_op jit(solution)/shard_map/pallas_call | solution.py:394
  23.5 0.5 %collective-permute-start.6 = (bf16[4,128,512]{2,1,0:T(8,128)(2,1)S(1)}, bf16[4,128,512]{2,1,0:T(8,128)(2,1)S(1)}, u32[]{:S(2)}, u32[]{:S(2)}) collective-permute-start(bf16[4,128,512]{2,1,0:T(8,128)(2,1)S(1)} %bitcast.7), channel_id=1, source_target_pairs={{0,16},{1,17},{2,18},{3,19},{4,20},{5,21},{6,22},{7,23},{8,24},{9,... | collective-permute-start | bytes 1572872 | tf_op jit(solution)/shard_map/ppermute | solution.py:57
  24.1 1.5 %collective-permute-done.6 = bf16[4,128,512]{2,1,0:T(8,128)(2,1)S(1)} collective-permute-done((bf16[4,128,512]{2,1,0:T(8,128)(2,1)S(1)}, bf16[4,128,512]{2,1,0:T(8,128)(2,1)S(1)}, u32[]{:S(2)}, u32[]{:S(2)}) %collective-permute-start.6) | collective-permute-done | bytes 524320 | tf_op jit(solution)/shard_map/ppermute | solution.py:57
  25.6 0.2 convert_add_fusion
  25.8 1.6 %collective-permute-start.7 = (bf16[2,128,512]{2,1,0:T(8,128)(2,1)S(1)}, bf16[2,128,512]{2,1,0:T(8,128)(2,1)S(1)}, u32[]{:S(2)}, u32[]{:S(2)}) collective-permute-start(bf16[2,128,512]{2,1,0:T(8,128)(2,1)S(1)} %slice.28), channel_id=1, source_target_pairs={{0,2},{1,3},{2,0},{3,1},{4,6},{5,7},{6,4},{7,5},{8,10},{9,11},{10,... | collective-permute-start | bytes 786440 | tf_op jit(solution)/shard_map/ppermute | solution.py:57
  27.5 4.8 %collective-permute-done.7 = bf16[2,128,512]{2,1,0:T(8,128)(2,1)S(1)} collective-permute-done((bf16[2,128,512]{2,1,0:T(8,128)(2,1)S(1)}, bf16[2,128,512]{2,1,0:T(8,128)(2,1)S(1)}, u32[]{:S(2)}, u32[]{:S(2)}) %collective-permute-start.7) | collective-permute-done | bytes 262176 | tf_op jit(solution)/shard_map/ppermute | solution.py:57
  32.3 0.1 slice_add_fusion
  32.4 2.7 %collective-permute-start.8 = (bf16[1,128,512]{2,1,0:T(8,128)(2,1)S(1)}, bf16[1,128,512]{2,1,0:T(8,128)(2,1)S(1)}, u32[]{:S(2)}, u32[]{:S(2)}) collective-permute-start(bf16[1,128,512]{2,1,0:T(8,128)(2,1)S(1)} %slice.29), channel_id=1, source_target_pairs={{0,8},{1,9},{2,10},{3,11},{4,12},{5,13},{6,14},{7,15},{8,0},{9,1},... | collective-permute-start | bytes 393224 | tf_op jit(solution)/shard_map/ppermute | solution.py:57
  35.1 4.6 %collective-permute-done.8 = bf16[1,128,512]{2,1,0:T(8,128)(2,1)S(1)} collective-permute-done((bf16[1,128,512]{2,1,0:T(8,128)(2,1)S(1)}, bf16[1,128,512]{2,1,0:T(8,128)(2,1)S(1)}, u32[]{:S(2)}, u32[]{:S(2)}) %collective-permute-start.8) | collective-permute-done | bytes 131104 | tf_op jit(solution)/shard_map/ppermute | solution.py:57
  39.7 0.7 %fusion = f32[1,128,512]{2,1,0:T(8,128)} fusion(f32[2,128,512]{2,1,0:T(8,128)S(1)} %slice_add_fusion, bf16[1,128,512]{2,1,0:T(8,128)(2,1)S(1)} %collective-permute-done.8), kind=kLoop, calls=%fused_computation.5 | loop fusion | flops 196608 | bytes 655360 | tf_op jit(solution)/shard_map/mul | solution.py:410
  (2 shorter events, 0.1 us)
Async XLA Ops:
  0.0 17.9 %collective-permute-start.5 = (bf16[1,2048,512]{2,1,0:T(8,128)(2,1)}, bf16[1,2048,512]{2,1,0:T(8,128)(2,1)S(1)}, u32[]{:S(2)}, u32[]{:S(2)}) collective-permute-start(bf16[1,2048,512]{2,1,0:T(8,128)(2,1)} %refs_0_.3), channel_id=1, source_target_pairs={{0,16},{1,17},{2,18},{3,19},{4,20},{5,21},{6,22},{7,23},{8,24},{9,... | collective-permute-start | bytes 6291464 | tf_op jit(solution)/shard_map/ppermute | solution.py:57
  1.6 6.9 %collective-permute-start = (bf16[64,2048]{1,0:T(8,128)(2,1)S(1)}, bf16[64,2048]{1,0:T(8,128)(2,1)S(1)}, u32[]{:S(2)}, u32[]{:S(2)}) collective-permute-start(bf16[64,2048]{1,0:T(8,128)(2,1)S(1)} %get-tuple-element.16.refs_2_), channel_id=1, source_target_pairs={{0,1},{1,0},{2,3},{3,2},{4,5},{5,4},{6,7},{7,6},{8,9},{9,8},{10,11... | collective-permute-start | bytes 786440 | tf_op jit(solution)/shard_map/ppermute | solution.py:57
  4.2 16.3 %collective-permute-start.1 = (bf16[64,2048]{1,0:T(8,128)(2,1)S(1)}, bf16[64,2048]{1,0:T(8,128)(2,1)S(1)}, u32[]{:S(2)}, u32[]{:S(2)}) collective-permute-start(bf16[64,2048]{1,0:T(8,128)(2,1)S(1)} %get-tuple-element.17), channel_id=1, source_target_pairs={{0,1},{1,0},{2,3},{3,2},{4,5},{5,4},{6,7},{7,6},{8,9},{9,8},{10,11... | collective-permute-start | bytes 786440 | tf_op jit(solution)/shard_map/ppermute | solution.py:57
  8.5 12.0 %collective-permute-start.2 = (bf16[64,2048]{1,0:T(8,128)(2,1)S(1)}, bf16[64,2048]{1,0:T(8,128)(2,1)S(1)}, u32[]{:S(2)}, u32[]{:S(2)}) collective-permute-start(bf16[64,2048]{1,0:T(8,128)(2,1)S(1)} %collective-permute-done.refs_0_), channel_id=1, source_target_pairs={{0,20},{1,21},{2,22},{3,23},{4,16},{5,17},{6,18},{7,19},{8,28},{9,... | collective-permute-start | bytes 786440 | tf_op jit(solution)/shard_map/ppermute | solution.py:57
  9.9 4.5 %collective-permute-start.3 = (f32[16,128]{1,0:T(8,128)S(1)}, f32[16,128]{1,0:T(8,128)S(1)}, u32[]{:S(2)}, u32[]{:S(2)}) collective-permute-start(f32[16,128]{1,0:T(8,128)S(1)} %get-tuple-element.18.refs_2_), channel_id=1, source_target_pairs={{0,20},{1,21},{2,22},{3,23},{4,16},{5,17},{6,18},{7,19},{8,28},{9,... | collective-permute-start | bytes 24584 | tf_op jit(solution)/shard_map/ppermute | solution.py:57
  14.4 3.5 %collective-permute-start.4 = (f32[16,128]{1,0:T(8,128)S(1)}, f32[16,128]{1,0:T(8,128)S(1)}, u32[]{:S(2)}, u32[]{:S(2)}) collective-permute-start(f32[16,128]{1,0:T(8,128)S(1)} %collective-permute-done.3.refs_0_), channel_id=1, source_target_pairs={{0,20},{1,21},{2,22},{3,23},{4,16},{5,17},{6,18},{7,19},{8,28},{9,... | collective-permute-start | bytes 24584 | tf_op jit(solution)/shard_map/ppermute | solution.py:57
  23.5 2.1 %collective-permute-start.6 = (bf16[4,128,512]{2,1,0:T(8,128)(2,1)S(1)}, bf16[4,128,512]{2,1,0:T(8,128)(2,1)S(1)}, u32[]{:S(2)}, u32[]{:S(2)}) collective-permute-start(bf16[4,128,512]{2,1,0:T(8,128)(2,1)S(1)} %bitcast.7), channel_id=1, source_target_pairs={{0,16},{1,17},{2,18},{3,19},{4,20},{5,21},{6,22},{7,23},{8,24},{9,... | collective-permute-start | bytes 1572872 | tf_op jit(solution)/shard_map/ppermute | solution.py:57
  25.8 6.4 %collective-permute-start.7 = (bf16[2,128,512]{2,1,0:T(8,128)(2,1)S(1)}, bf16[2,128,512]{2,1,0:T(8,128)(2,1)S(1)}, u32[]{:S(2)}, u32[]{:S(2)}) collective-permute-start(bf16[2,128,512]{2,1,0:T(8,128)(2,1)S(1)} %slice.28), channel_id=1, source_target_pairs={{0,2},{1,3},{2,0},{3,1},{4,6},{5,7},{6,4},{7,5},{8,10},{9,11},{10,... | collective-permute-start | bytes 786440 | tf_op jit(solution)/shard_map/ppermute | solution.py:57
  32.4 7.3 %collective-permute-start.8 = (bf16[1,128,512]{2,1,0:T(8,128)(2,1)S(1)}, bf16[1,128,512]{2,1,0:T(8,128)(2,1)S(1)}, u32[]{:S(2)}, u32[]{:S(2)}) collective-permute-start(bf16[1,128,512]{2,1,0:T(8,128)(2,1)S(1)} %slice.29), channel_id=1, source_target_pairs={{0,8},{1,9},{2,10},{3,11},{4,12},{5,13},{6,14},{7,15},{8,0},{9,1},... | collective-permute-start | bytes 393224 | tf_op jit(solution)/shard_map/ppermute | solution.py:57

commit v2 on v1

--- a/solution.py
+++ b/solution.py
@@ -392,22 +392,48 @@
             compiler_params=limit,
         )
         outs = backward(*given, streams, hiddens, inputs, scales, *held, *outs)
+
+    def split_sum(total, came):
+        half = total.shape[0] // 2
+        return pl.pallas_call(
+            split_sum_kernel,
+            out_shape=(pltpu.VMEM((half, block, rank), f32), pltpu.VMEM((half, block, rank), bf16)),
+            in_specs=[in_vmem] * 2,
+            out_specs=(in_vmem,) * 2,
+            compiler_params=limit,
+        )(total, pltpu.with_memory_space_constraint(came, pltpu.VMEM))
+
+    def swap(array, turn):
+        return permute(array, plan, lambda section, replica: ((section + turn) % sections, replica))
+
     total = outs[0]
-    for turn in range(1, sections):
-        total = total + permute(
-            outs[1][turn - 1], plan, lambda section, replica: ((section + turn) % sections, replica)
-        ).astype(f32)
-    left = plan.blocks
-    stage = 0
-    while left > 1:
-        left //= 2
+    if sections == 2:
+        came = swap(outs[1][0], 1)
+    else:
+        for turn in range(1, sections):
+            total = total + swap(outs[1][turn - 1], turn).astype(f32)
+    for stage in range(len(plan.summed)):
 
         def route(section, replica):
             return section, replica ^ (1 << plan.order(section)[stage])
 
-        total = total[:left] + permute(total[left:].astype(bf16), plan, route).astype(f32)
-        stage += 1
+        if sections == 2:
+            total, leaving = split_sum(total, came)
+        else:
+            half = total.shape[0] // 2
+            total, leaving = total[:half], total[half:].astype(bf16)
+        came = permute(leaving, plan, route)
+        if sections != 2:
+            total = total + came.astype(f32)
+    if sections == 2:
+        total = total + came.astype(f32)
     return total * (1.0 / math.sqrt(points * replicas))
+
+
+def split_sum_kernel(total, came, kept, leaving):
+    half = kept.shape[0]
+    kept[...] = total[:half] + came[:half].astype(jnp.float32)
+    leaving[...] = (total[half:] + came[half:].astype(jnp.float32)).astype(jnp.bfloat16)
 
 
 def solution(mesh):

time: 40.6 us -> 40.4 us (level)
  no operation moved by 1% of the time
where the time goes in v2:
time: 40.4 us; the launch traced here: 40.3 us
  waiting for transfers between devices  17.8 us (44%)
  starting transfers between devices  12.9 us (32%)
  Pallas kernels  8.66 us (21%)
  other arithmetic  0.74 us (2%)
    ppermute x9, waiting for transfers between devices, permute(): return lax.ppermute(block, AXES, pairs)  17.8 us
    ppermute x9, starting transfers between devices, permute(): return lax.ppermute(block, AXES, pairs)  12.9 us
    pallas_call x1, Pallas kernels, on_device(): outs = backward(*given, streams, hiddens, inputs, scales, *held, *outs)  2.99 us
    pallas_call x1, Pallas kernels, on_device(): streams, hiddens, inputs, scales = forward(*small_units, table, *held)  2.63 us
    pallas_call x1, Pallas kernels, on_device(): table, held = load(in_hbm(node_table), *weights[:plan.loads])  1.78 us
    pallas_call x1, Pallas kernels, on_device(): small, *halves = prepare(*map(in_hbm, (*arrays, flat_upstream)))  1.12 us
  transfers between devices with their start and end apart: 9, of which 5 were waited for; matrix products, arithmetic and copies ran while one was open for 0% of the time, Pallas kernels for 14%

profile of v2, /device:TPU:0, one launch (start us, length us, event | category | flops | bytes accessed | tf_op | source)
XLA Modules:
  0.0 40.3 jit_solution(18060171000776338729)
XLA Ops:
  0.0 0.5 %collective-permute-start.5 = (bf16[1,2048,512]{2,1,0:T(8,128)(2,1)}, bf16[1,2048,512]{2,1,0:T(8,128)(2,1)S(1)}, u32[]{:S(2)}, u32[]{:S(2)}) collective-permute-start(bf16[1,2048,512]{2,1,0:T(8,128)(2,1)} %refs_0_.3), channel_id=1, source_target_pairs={{0,16},{1,17},{2,18},{3,19},{4,20},{5,21},{6,22},{7,23},{8,24},{9,... | collective-permute-start | bytes 6291464 | tf_op jit(solution)/shard_map/ppermute | solution.py:57
  0.5 1.1 %prepare.1 = (f32[16,128]{1,0:T(8,128)S(1)}, bf16[64,2048]{1,0:T(8,128)(2,1)S(1)}, bf16[64,2048]{1,0:T(8,128)(2,1)S(1)}) custom-call(s32[4,32]{1,0:T(4,128)} %refs_0_.2, s32[4,8,32]{2,1,0:T(8,128)} %bitcast.9, f32[4,8,32]{2,1,0:T(8,128)} %bitcast.10, bf16[128,2048]{1,0:T(8,128)(2,1)} %bitcast.8), custom_call_target="tpu_custom_call" | custom-call | tf_op jit(solution)/shard_map/prepare/pallas_call | solution.py:301
  1.6 2.5 %collective-permute-start = (bf16[64,2048]{1,0:T(8,128)(2,1)S(1)}, bf16[64,2048]{1,0:T(8,128)(2,1)S(1)}, u32[]{:S(2)}, u32[]{:S(2)}) collective-permute-start(bf16[64,2048]{1,0:T(8,128)(2,1)S(1)} %get-tuple-element.20.refs_2_), channel_id=1, source_target_pairs={{0,1},{1,0},{2,3},{3,2},{4,5},{5,4},{6,7},{7,6},{8,9},{9,8},{10,11... | collective-permute-start | bytes 786440 | tf_op jit(solution)/shard_map/ppermute | solution.py:57
  4.2 0.1 collective-permute-start.1
  4.2 4.3 %collective-permute-done.refs_0_ = bf16[64,2048]{1,0:T(8,128)(2,1)S(1)} collective-permute-done((bf16[64,2048]{1,0:T(8,128)(2,1)S(1)}, bf16[64,2048]{1,0:T(8,128)(2,1)S(1)}, u32[]{:S(2)}, u32[]{:S(2)}) %collective-permute-start) | collective-permute-done | bytes 262176 | tf_op jit(solution)/shard_map/ppermute | solution.py:57
  8.5 1.4 %collective-permute-start.2 = (bf16[64,2048]{1,0:T(8,128)(2,1)S(1)}, bf16[64,2048]{1,0:T(8,128)(2,1)S(1)}, u32[]{:S(2)}, u32[]{:S(2)}) collective-permute-start(bf16[64,2048]{1,0:T(8,128)(2,1)S(1)} %collective-permute-done.refs_0_), channel_id=1, source_target_pairs={{0,20},{1,21},{2,22},{3,23},{4,16},{5,17},{6,18},{7,19},{8,28},{9,... | collective-permute-start | bytes 786440 | tf_op jit(solution)/shard_map/ppermute | solution.py:57
  9.9 2.0 %collective-permute-start.3 = (f32[16,128]{1,0:T(8,128)S(1)}, f32[16,128]{1,0:T(8,128)S(1)}, u32[]{:S(2)}, u32[]{:S(2)}) collective-permute-start(f32[16,128]{1,0:T(8,128)S(1)} %get-tuple-element.22.refs_2_), channel_id=1, source_target_pairs={{0,20},{1,21},{2,22},{3,23},{4,16},{5,17},{6,18},{7,19},{8,28},{9,... | collective-permute-start | bytes 24584 | tf_op jit(solution)/shard_map/ppermute | solution.py:57
  11.8 2.6 %collective-permute-done.3.refs_0_ = f32[16,128]{1,0:T(8,128)S(1)} collective-permute-done((f32[16,128]{1,0:T(8,128)S(1)}, f32[16,128]{1,0:T(8,128)S(1)}, u32[]{:S(2)}, u32[]{:S(2)}) %collective-permute-start.3) | collective-permute-done | bytes 8224 | tf_op jit(solution)/shard_map/ppermute | solution.py:57
  14.4 1.7 %collective-permute-start.4 = (f32[16,128]{1,0:T(8,128)S(1)}, f32[16,128]{1,0:T(8,128)S(1)}, u32[]{:S(2)}, u32[]{:S(2)}) collective-permute-start(f32[16,128]{1,0:T(8,128)S(1)} %collective-permute-done.3.refs_0_), channel_id=1, source_target_pairs={{0,20},{1,21},{2,22},{3,23},{4,16},{5,17},{6,18},{7,19},{8,28},{9,... | collective-permute-start | bytes 24584 | tf_op jit(solution)/shard_map/ppermute | solution.py:57
  16.1 1.8 %load.1 = (bf16[128,2048]{1,0:T(8,128)(2,1)S(1)}, bf16[2048,512]{1,0:T(8,128)(2,1)S(1)}) custom-call(bf16[128,2048]{1,0:T(8,128)(2,1)} %table.1, bf16[1,2048,512]{2,1,0:T(8,128)(2,1)} %refs_0_.3), custom_call_target="tpu_custom_call" | custom-call | tf_op jit(solution)/shard_map/load/pallas_call | solution.py:367
  17.9 0.0 collective-permute-done.4.refs_1_
  17.9 0.0 collective-permute-done.5
  17.9 2.6 %forward.1 = (bf16[2,256,2048]{2,1,0:T(8,128)(2,1)S(1)}, bf16[2,256,512]{2,1,0:T(8,128)(2,1)S(1)}, f32[2,256,512]{2,1,0:T(8,128)S(1)}, f32[2,256,128]{2,1,0:T(8,128)S(1)}) custom-call(f32[16,128]{1,0:T(8,128)S(1)} %collective-permute-done.3.refs_0_, f32[16,128]{1,0:T(8,128)S(1)} %collective-permute-done.4.refs_1_, f32[16,128]{1,0:T(8,128)S(1)} %get-tuple-element.22.refs_2_, ...), custom_call_target="tpu_custom_call" | custom-call | flops 2147483648 | bytes 6291456 | tf_op jit(solution)/shard_map/forward/pallas_call | solution.py:369
  20.5 0.0 collective-permute-done.1.refs_1_
  20.5 0.0 collective-permute-done.2.refs_3_
  20.5 3.0 %shard_map.64 = (f32[4,128,512]{2,1,0:T(8,128)S(1)}, bf16[1,4,128,512]{3,2,1,0:T(8,128)(2,1)S(1)}) custom-call(bf16[64,2048]{1,0:T(8,128)(2,1)S(1)} %collective-permute-done.refs_0_, bf16[64,2048]{1,0:T(8,128)(2,1)S(1)} %collective-permute-done.1.refs_1_, bf16[64,2048]{1,0:T(8,128)(2,1)S(1)} %get-tuple-element.20.refs_2_, ...), custom_call_target="tpu_custom_call" | custom-call | flops 3221225472 | bytes 6291456 | tf_op jit(solution)/shard_map/pallas_call | solution.py:394
  23.5 0.5 %collective-permute-start.6 = (bf16[4,128,512]{2,1,0:T(8,128)(2,1)S(1)}, bf16[4,128,512]{2,1,0:T(8,128)(2,1)S(1)}, u32[]{:S(2)}, u32[]{:S(2)}) collective-permute-start(bf16[4,128,512]{2,1,0:T(8,128)(2,1)S(1)} %bitcast.7), channel_id=1, source_target_pairs={{0,16},{1,17},{2,18},{3,19},{4,20},{5,21},{6,22},{7,23},{8,24},{9,... | collective-permute-start | bytes 1572872 | tf_op jit(solution)/shard_map/ppermute | solution.py:57
  24.1 1.5 %collective-permute-done.6.came = bf16[4,128,512]{2,1,0:T(8,128)(2,1)S(1)} collective-permute-done((bf16[4,128,512]{2,1,0:T(8,128)(2,1)S(1)}, bf16[4,128,512]{2,1,0:T(8,128)(2,1)S(1)}, u32[]{:S(2)}, u32[]{:S(2)}) %collective-permute-start.6) | collective-permute-done | bytes 524320 | tf_op jit(solution)/shard_map/ppermute | solution.py:57
  25.6 0.1 shard_map.65
  25.7 1.6 %collective-permute-start.7 = (bf16[2,128,512]{2,1,0:T(8,128)(2,1)S(1)}, bf16[2,128,512]{2,1,0:T(8,128)(2,1)S(1)}, u32[]{:S(2)}, u32[]{:S(2)}) collective-permute-start(bf16[2,128,512]{2,1,0:T(8,128)(2,1)S(1)} %get-tuple-element.32), channel_id=1, source_target_pairs={{0,2},{1,3},{2,0},{3,1},{4,6},{5,7},{6,4},{7,5},{8,10},{9,11},{10,... | collective-permute-start | bytes 786440 | tf_op jit(solution)/shard_map/ppermute | solution.py:57
  27.3 4.8 %collective-permute-done.7.came = bf16[2,128,512]{2,1,0:T(8,128)(2,1)S(1)} collective-permute-done((bf16[2,128,512]{2,1,0:T(8,128)(2,1)S(1)}, bf16[2,128,512]{2,1,0:T(8,128)(2,1)S(1)}, u32[]{:S(2)}, u32[]{:S(2)}) %collective-permute-start.7) | collective-permute-done | bytes 262176 | tf_op jit(solution)/shard_map/ppermute | solution.py:57
  32.2 2.7 %collective-permute-start.8 = (bf16[1,128,512]{2,1,0:T(8,128)(2,1)S(1)}, bf16[1,128,512]{2,1,0:T(8,128)(2,1)S(1)}, u32[]{:S(2)}, u32[]{:S(2)}) collective-permute-start(bf16[1,128,512]{2,1,0:T(8,128)(2,1)S(1)} %get-tuple-element.34), channel_id=1, source_target_pairs={{0,8},{1,9},{2,10},{3,11},{4,12},{5,13},{6,14},{7,15},{8,0},{9,1},... | collective-permute-start | bytes 393224 | tf_op jit(solution)/shard_map/ppermute | solution.py:57
  34.9 4.6 %collective-permute-done.8 = bf16[1,128,512]{2,1,0:T(8,128)(2,1)S(1)} collective-permute-done((bf16[1,128,512]{2,1,0:T(8,128)(2,1)S(1)}, bf16[1,128,512]{2,1,0:T(8,128)(2,1)S(1)}, u32[]{:S(2)}, u32[]{:S(2)}) %collective-permute-start.8) | collective-permute-done | bytes 131104 | tf_op jit(solution)/shard_map/ppermute | solution.py:57
  39.5 0.7 %add_multiply_fusion = f32[1,128,512]{2,1,0:T(8,128)} fusion(f32[1,128,512]{2,1,0:T(8,128)S(1)} %get-tuple-element.33, bf16[1,128,512]{2,1,0:T(8,128)(2,1)S(1)} %collective-permute-done.8), kind=kLoop, calls=%fused_computation | loop fusion | flops 196608 | bytes 655360 | tf_op jit(solution)/shard_map/mul | solution.py:430
  (1 shorter events, 0.0 us)
Async XLA Ops:
  0.0 17.9 %collective-permute-start.5 = (bf16[1,2048,512]{2,1,0:T(8,128)(2,1)}, bf16[1,2048,512]{2,1,0:T(8,128)(2,1)S(1)}, u32[]{:S(2)}, u32[]{:S(2)}) collective-permute-start(bf16[1,2048,512]{2,1,0:T(8,128)(2,1)} %refs_0_.3), channel_id=1, source_target_pairs={{0,16},{1,17},{2,18},{3,19},{4,20},{5,21},{6,22},{7,23},{8,24},{9,... | collective-permute-start | bytes 6291464 | tf_op jit(solution)/shard_map/ppermute | solution.py:57
  1.6 6.9 %collective-permute-start = (bf16[64,2048]{1,0:T(8,128)(2,1)S(1)}, bf16[64,2048]{1,0:T(8,128)(2,1)S(1)}, u32[]{:S(2)}, u32[]{:S(2)}) collective-permute-start(bf16[64,2048]{1,0:T(8,128)(2,1)S(1)} %get-tuple-element.20.refs_2_), channel_id=1, source_target_pairs={{0,1},{1,0},{2,3},{3,2},{4,5},{5,4},{6,7},{7,6},{8,9},{9,8},{10,11... | collective-permute-start | bytes 786440 | tf_op jit(solution)/shard_map/ppermute | solution.py:57
  4.2 16.3 %collective-permute-start.1 = (bf16[64,2048]{1,0:T(8,128)(2,1)S(1)}, bf16[64,2048]{1,0:T(8,128)(2,1)S(1)}, u32[]{:S(2)}, u32[]{:S(2)}) collective-permute-start(bf16[64,2048]{1,0:T(8,128)(2,1)S(1)} %get-tuple-element.21), channel_id=1, source_target_pairs={{0,1},{1,0},{2,3},{3,2},{4,5},{5,4},{6,7},{7,6},{8,9},{9,8},{10,11... | collective-permute-start | bytes 786440 | tf_op jit(solution)/shard_map/ppermute | solution.py:57
  8.5 12.0 %collective-permute-start.2 = (bf16[64,2048]{1,0:T(8,128)(2,1)S(1)}, bf16[64,2048]{1,0:T(8,128)(2,1)S(1)}, u32[]{:S(2)}, u32[]{:S(2)}) collective-permute-start(bf16[64,2048]{1,0:T(8,128)(2,1)S(1)} %collective-permute-done.refs_0_), channel_id=1, source_target_pairs={{0,20},{1,21},{2,22},{3,23},{4,16},{5,17},{6,18},{7,19},{8,28},{9,... | collective-permute-start | bytes 786440 | tf_op jit(solution)/shard_map/ppermute | solution.py:57
  9.9 4.5 %collective-permute-start.3 = (f32[16,128]{1,0:T(8,128)S(1)}, f32[16,128]{1,0:T(8,128)S(1)}, u32[]{:S(2)}, u32[]{:S(2)}) collective-permute-start(f32[16,128]{1,0:T(8,128)S(1)} %get-tuple-element.22.refs_2_), channel_id=1, source_target_pairs={{0,20},{1,21},{2,22},{3,23},{4,16},{5,17},{6,18},{7,19},{8,28},{9,... | collective-permute-start | bytes 24584 | tf_op jit(solution)/shard_map/ppermute | solution.py:57
  14.4 3.5 %collective-permute-start.4 = (f32[16,128]{1,0:T(8,128)S(1)}, f32[16,128]{1,0:T(8,128)S(1)}, u32[]{:S(2)}, u32[]{:S(2)}) collective-permute-start(f32[16,128]{1,0:T(8,128)S(1)} %collective-permute-done.3.refs_0_), channel_id=1, source_target_pairs={{0,20},{1,21},{2,22},{3,23},{4,16},{5,17},{6,18},{7,19},{8,28},{9,... | collective-permute-start | bytes 24584 | tf_op jit(solution)/shard_map/ppermute | solution.py:57
  23.5 2.1 %collective-permute-start.6 = (bf16[4,128,512]{2,1,0:T(8,128)(2,1)S(1)}, bf16[4,128,512]{2,1,0:T(8,128)(2,1)S(1)}, u32[]{:S(2)}, u32[]{:S(2)}) collective-permute-start(bf16[4,128,512]{2,1,0:T(8,128)(2,1)S(1)} %bitcast.7), channel_id=1, source_target_pairs={{0,16},{1,17},{2,18},{3,19},{4,20},{5,21},{6,22},{7,23},{8,24},{9,... | collective-permute-start | bytes 1572872 | tf_op jit(solution)/shard_map/ppermute | solution.py:57
  25.7 6.4 %collective-permute-start.7 = (bf16[2,128,512]{2,1,0:T(8,128)(2,1)S(1)}, bf16[2,128,512]{2,1,0:T(8,128)(2,1)S(1)}, u32[]{:S(2)}, u32[]{:S(2)}) collective-permute-start(bf16[2,128,512]{2,1,0:T(8,128)(2,1)S(1)} %get-tuple-element.32), channel_id=1, source_target_pairs={{0,2},{1,3},{2,0},{3,1},{4,6},{5,7},{6,4},{7,5},{8,10},{9,11},{10,... | collective-permute-start | bytes 786440 | tf_op jit(solution)/shard_map/ppermute | solution.py:57
  32.2 7.3 %collective-permute-start.8 = (bf16[1,128,512]{2,1,0:T(8,128)(2,1)S(1)}, bf16[1,128,512]{2,1,0:T(8,128)(2,1)S(1)}, u32[]{:S(2)}, u32[]{:S(2)}) collective-permute-start(bf16[1,128,512]{2,1,0:T(8,128)(2,1)S(1)} %get-tuple-element.34), channel_id=1, source_target_pairs={{0,8},{1,9},{2,10},{3,11},{4,12},{5,13},{6,14},{7,15},{8,0},{9,1},... | collective-permute-start | bytes 393224 | tf_op jit(solution)/shard_map/ppermute | solution.py:57

commit v3 on v2

--- a/solution.py
+++ b/solution.py
@@ -14,6 +14,7 @@
 AXES = ("section", "dp")
 SHARED_BITS = (0, 2)
 LIMIT = 36 << 20
+PARTS = 2
 
 
 def mask_of(number, bits):
@@ -425,9 +426,30 @@
         came = permute(leaving, plan, route)
         if sections != 2:
             total = total + came.astype(f32)
-    if sections == 2:
-        total = total + came.astype(f32)
-    return total * (1.0 / math.sqrt(points * replicas))
+    factor = 1.0 / math.sqrt(points * replicas)
+    if sections != 2:
+        return total * factor
+    return pl.pallas_call(
+        functools.partial(finish_kernel, factor),
+        out_shape=jax.ShapeDtypeStruct(total.shape, f32),
+        in_specs=[in_vmem] * 2,
+        out_specs=anywhere,
+        scratch_shapes=[pltpu.VMEM(total.shape, f32), pltpu.SemaphoreType.DMA((PARTS,))],
+        compiler_params=limit,
+        name="finish",
+    )(total, pltpu.with_memory_space_constraint(came, pltpu.VMEM))
+
+
+def finish_kernel(factor, total, came, out, held, sem):
+    size = total.shape[1] // PARTS
+    copies = []
+    for i in range(PARTS):
+        rows = pl.ds(i * size, size)
+        held[:, rows, :] = (total[:, rows, :] + came[:, rows, :].astype(jnp.float32)) * factor
+        copies.append(pltpu.make_async_copy(held.at[:, rows], out.at[:, rows], sem.at[i]))
+        copies[-1].start()
+    for copy in copies:
+        copy.wait()
 
 
 def split_sum_kernel(total, came, kept, leaving):

time: 40.4 us -> 40.4 us (level)
  other arithmetic: 0.74 us -> 0 us
  Pallas kernels: 8.66 us -> 9.39 us
    mul x1 -> x0, other arithmetic: 0.74 us -> none  [on_device(): return total * (1.0 / math.sqrt(points * replicas))]
    pallas_call x0 -> x1, Pallas kernels: none -> 0.73 us  [on_device(): pl.pallas_call(functools.partial(finish_kernel, factor), out_shape=jax.Sh...]
where the time goes in v3:
time: 40.4 us; the launch traced here: 40.3 us
  waiting for transfers between devices  17.8 us (44%)
  starting transfers between devices  12.9 us (32%)
  Pallas kernels  9.39 us (23%)
    ppermute x9, waiting for transfers between devices, permute(): return lax.ppermute(block, AXES, pairs)  17.8 us
    ppermute x9, starting transfers between devices, permute(): return lax.ppermute(block, AXES, pairs)  12.9 us
    pallas_call x1, Pallas kernels, on_device(): outs = backward(*given, streams, hiddens, inputs, scales, *held, *outs)  2.99 us
    pallas_call x1, Pallas kernels, on_device(): streams, hiddens, inputs, scales = forward(*small_units, table, *held)  2.63 us
    pallas_call x1, Pallas kernels, on_device(): table, held = load(in_hbm(node_table), *weights[:plan.loads])  1.78 us
    pallas_call x1, Pallas kernels, on_device(): small, *halves = prepare(*map(in_hbm, (*arrays, flat_upstream)))  1.12 us
  transfers between devices with their start and end apart: 9, of which 5 were waited for; matrix products, arithmetic and copies ran while one was open for 0% of the time, Pallas kernels for 14%

profile of v3, /device:TPU:0, one launch (start us, length us, event | category | flops | bytes accessed | tf_op | source)
XLA Modules:
  0.0 40.3 jit_solution(16252693838952026383)
XLA Ops:
  0.0 0.5 %collective-permute-start.5 = (bf16[1,2048,512]{2,1,0:T(8,128)(2,1)}, bf16[1,2048,512]{2,1,0:T(8,128)(2,1)S(1)}, u32[]{:S(2)}, u32[]{:S(2)}) collective-permute-start(bf16[1,2048,512]{2,1,0:T(8,128)(2,1)} %refs_0_.3), channel_id=1, source_target_pairs={{0,16},{1,17},{2,18},{3,19},{4,20},{5,21},{6,22},{7,23},{8,24},{9,... | collective-permute-start | bytes 6291464 | tf_op jit(solution)/shard_map/ppermute | solution.py:58
  0.5 1.1 %prepare.1 = (f32[16,128]{1,0:T(8,128)S(1)}, bf16[64,2048]{1,0:T(8,128)(2,1)S(1)}, bf16[64,2048]{1,0:T(8,128)(2,1)S(1)}) custom-call(s32[4,32]{1,0:T(4,128)} %refs_0_.2, s32[4,8,32]{2,1,0:T(8,128)} %bitcast.9, f32[4,8,32]{2,1,0:T(8,128)} %bitcast.10, bf16[128,2048]{1,0:T(8,128)(2,1)} %bitcast.8), custom_call_target="tpu_custom_call" | custom-call | tf_op jit(solution)/shard_map/prepare/pallas_call | solution.py:302
  1.6 2.5 %collective-permute-start = (bf16[64,2048]{1,0:T(8,128)(2,1)S(1)}, bf16[64,2048]{1,0:T(8,128)(2,1)S(1)}, u32[]{:S(2)}, u32[]{:S(2)}) collective-permute-start(bf16[64,2048]{1,0:T(8,128)(2,1)S(1)} %get-tuple-element.20.refs_2_), channel_id=1, source_target_pairs={{0,1},{1,0},{2,3},{3,2},{4,5},{5,4},{6,7},{7,6},{8,9},{9,8},{10,11... | collective-permute-start | bytes 786440 | tf_op jit(solution)/shard_map/ppermute | solution.py:58
  4.2 0.1 collective-permute-start.1
  4.2 4.3 %collective-permute-done.refs_0_ = bf16[64,2048]{1,0:T(8,128)(2,1)S(1)} collective-permute-done((bf16[64,2048]{1,0:T(8,128)(2,1)S(1)}, bf16[64,2048]{1,0:T(8,128)(2,1)S(1)}, u32[]{:S(2)}, u32[]{:S(2)}) %collective-permute-start) | collective-permute-done | bytes 262176 | tf_op jit(solution)/shard_map/ppermute | solution.py:58
  8.5 1.4 %collective-permute-start.2 = (bf16[64,2048]{1,0:T(8,128)(2,1)S(1)}, bf16[64,2048]{1,0:T(8,128)(2,1)S(1)}, u32[]{:S(2)}, u32[]{:S(2)}) collective-permute-start(bf16[64,2048]{1,0:T(8,128)(2,1)S(1)} %collective-permute-done.refs_0_), channel_id=1, source_target_pairs={{0,20},{1,21},{2,22},{3,23},{4,16},{5,17},{6,18},{7,19},{8,28},{9,... | collective-permute-start | bytes 786440 | tf_op jit(solution)/shard_map/ppermute | solution.py:58
  9.9 2.0 %collective-permute-start.3 = (f32[16,128]{1,0:T(8,128)S(1)}, f32[16,128]{1,0:T(8,128)S(1)}, u32[]{:S(2)}, u32[]{:S(2)}) collective-permute-start(f32[16,128]{1,0:T(8,128)S(1)} %get-tuple-element.22.refs_2_), channel_id=1, source_target_pairs={{0,20},{1,21},{2,22},{3,23},{4,16},{5,17},{6,18},{7,19},{8,28},{9,... | collective-permute-start | bytes 24584 | tf_op jit(solution)/shard_map/ppermute | solution.py:58
  11.8 2.6 %collective-permute-done.3.refs_0_ = f32[16,128]{1,0:T(8,128)S(1)} collective-permute-done((f32[16,128]{1,0:T(8,128)S(1)}, f32[16,128]{1,0:T(8,128)S(1)}, u32[]{:S(2)}, u32[]{:S(2)}) %collective-permute-start.3) | collective-permute-done | bytes 8224 | tf_op jit(solution)/shard_map/ppermute | solution.py:58
  14.4 1.7 %collective-permute-start.4 = (f32[16,128]{1,0:T(8,128)S(1)}, f32[16,128]{1,0:T(8,128)S(1)}, u32[]{:S(2)}, u32[]{:S(2)}) collective-permute-start(f32[16,128]{1,0:T(8,128)S(1)} %collective-permute-done.3.refs_0_), channel_id=1, source_target_pairs={{0,20},{1,21},{2,22},{3,23},{4,16},{5,17},{6,18},{7,19},{8,28},{9,... | collective-permute-start | bytes 24584 | tf_op jit(solution)/shard_map/ppermute | solution.py:58
  16.1 1.8 %load.1 = (bf16[128,2048]{1,0:T(8,128)(2,1)S(1)}, bf16[2048,512]{1,0:T(8,128)(2,1)S(1)}) custom-call(bf16[128,2048]{1,0:T(8,128)(2,1)} %table.1, bf16[1,2048,512]{2,1,0:T(8,128)(2,1)} %refs_0_.3), custom_call_target="tpu_custom_call" | custom-call | tf_op jit(solution)/shard_map/load/pallas_call | solution.py:368
  17.9 0.0 collective-permute-done.4.refs_1_
  17.9 0.0 collective-permute-done.5
  17.9 2.6 %forward.1 = (bf16[2,256,2048]{2,1,0:T(8,128)(2,1)S(1)}, bf16[2,256,512]{2,1,0:T(8,128)(2,1)S(1)}, f32[2,256,512]{2,1,0:T(8,128)S(1)}, f32[2,256,128]{2,1,0:T(8,128)S(1)}) custom-call(f32[16,128]{1,0:T(8,128)S(1)} %collective-permute-done.3.refs_0_, f32[16,128]{1,0:T(8,128)S(1)} %collective-permute-done.4.refs_1_, f32[16,128]{1,0:T(8,128)S(1)} %get-tuple-element.22.refs_2_, ...), custom_call_target="tpu_custom_call" | custom-call | flops 2147483648 | bytes 6291456 | tf_op jit(solution)/shard_map/forward/pallas_call | solution.py:370
  20.5 0.0 collective-permute-done.1.refs_1_
  20.5 0.0 collective-permute-done.2.refs_3_
  20.5 3.0 %shard_map.64 = (f32[4,128,512]{2,1,0:T(8,128)S(1)}, bf16[1,4,128,512]{3,2,1,0:T(8,128)(2,1)S(1)}) custom-call(bf16[64,2048]{1,0:T(8,128)(2,1)S(1)} %collective-permute-done.refs_0_, bf16[64,2048]{1,0:T(8,128)(2,1)S(1)} %collective-permute-done.1.refs_1_, bf16[64,2048]{1,0:T(8,128)(2,1)S(1)} %get-tuple-element.20.refs_2_, ...), custom_call_target="tpu_custom_call" | custom-call | flops 3221225472 | bytes 6291456 | tf_op jit(solution)/shard_map/pallas_call | solution.py:395
  23.5 0.5 %collective-permute-start.6 = (bf16[4,128,512]{2,1,0:T(8,128)(2,1)S(1)}, bf16[4,128,512]{2,1,0:T(8,128)(2,1)S(1)}, u32[]{:S(2)}, u32[]{:S(2)}) collective-permute-start(bf16[4,128,512]{2,1,0:T(8,128)(2,1)S(1)} %bitcast.7), channel_id=1, source_target_pairs={{0,16},{1,17},{2,18},{3,19},{4,20},{5,21},{6,22},{7,23},{8,24},{9,... | collective-permute-start | bytes 1572872 | tf_op jit(solution)/shard_map/ppermute | solution.py:58
  24.1 1.5 %collective-permute-done.6.came = bf16[4,128,512]{2,1,0:T(8,128)(2,1)S(1)} collective-permute-done((bf16[4,128,512]{2,1,0:T(8,128)(2,1)S(1)}, bf16[4,128,512]{2,1,0:T(8,128)(2,1)S(1)}, u32[]{:S(2)}, u32[]{:S(2)}) %collective-permute-start.6) | collective-permute-done | bytes 524320 | tf_op jit(solution)/shard_map/ppermute | solution.py:58
  25.6 0.1 shard_map.65
  25.7 1.6 %collective-permute-start.7 = (bf16[2,128,512]{2,1,0:T(8,128)(2,1)S(1)}, bf16[2,128,512]{2,1,0:T(8,128)(2,1)S(1)}, u32[]{:S(2)}, u32[]{:S(2)}) collective-permute-start(bf16[2,128,512]{2,1,0:T(8,128)(2,1)S(1)} %get-tuple-element.32), channel_id=1, source_target_pairs={{0,2},{1,3},{2,0},{3,1},{4,6},{5,7},{6,4},{7,5},{8,10},{9,11},{10,... | collective-permute-start | bytes 786440 | tf_op jit(solution)/shard_map/ppermute | solution.py:58
  27.3 4.8 %collective-permute-done.7.came = bf16[2,128,512]{2,1,0:T(8,128)(2,1)S(1)} collective-permute-done((bf16[2,128,512]{2,1,0:T(8,128)(2,1)S(1)}, bf16[2,128,512]{2,1,0:T(8,128)(2,1)S(1)}, u32[]{:S(2)}, u32[]{:S(2)}) %collective-permute-start.7) | collective-permute-done | bytes 262176 | tf_op jit(solution)/shard_map/ppermute | solution.py:58
  32.2 2.7 %collective-permute-start.8 = (bf16[1,128,512]{2,1,0:T(8,128)(2,1)S(1)}, bf16[1,128,512]{2,1,0:T(8,128)(2,1)S(1)}, u32[]{:S(2)}, u32[]{:S(2)}) collective-permute-start(bf16[1,128,512]{2,1,0:T(8,128)(2,1)S(1)} %get-tuple-element.34), channel_id=1, source_target_pairs={{0,8},{1,9},{2,10},{3,11},{4,12},{5,13},{6,14},{7,15},{8,0},{9,1},... | collective-permute-start | bytes 393224 | tf_op jit(solution)/shard_map/ppermute | solution.py:58
  34.9 4.6 %collective-permute-done.8.came = bf16[1,128,512]{2,1,0:T(8,128)(2,1)S(1)} collective-permute-done((bf16[1,128,512]{2,1,0:T(8,128)(2,1)S(1)}, bf16[1,128,512]{2,1,0:T(8,128)(2,1)S(1)}, u32[]{:S(2)}, u32[]{:S(2)}) %collective-permute-start.8) | collective-permute-done | bytes 131104 | tf_op jit(solution)/shard_map/ppermute | solution.py:58
  39.5 0.7 %finish.1 = f32[1,128,512]{2,1,0:T(8,128)} custom-call(f32[1,128,512]{2,1,0:T(8,128)S(1)} %get-tuple-element.33.total, bf16[1,128,512]{2,1,0:T(8,128)(2,1)S(1)} %collective-permute-done.8.came), custom_call_target="tpu_custom_call" | custom-call | tf_op jit(solution)/shard_map/finish/pallas_call | solution.py:432
  (1 shorter events, 0.0 us)
Async XLA Ops:
  0.0 17.9 %collective-permute-start.5 = (bf16[1,2048,512]{2,1,0:T(8,128)(2,1)}, bf16[1,2048,512]{2,1,0:T(8,128)(2,1)S(1)}, u32[]{:S(2)}, u32[]{:S(2)}) collective-permute-start(bf16[1,2048,512]{2,1,0:T(8,128)(2,1)} %refs_0_.3), channel_id=1, source_target_pairs={{0,16},{1,17},{2,18},{3,19},{4,20},{5,21},{6,22},{7,23},{8,24},{9,... | collective-permute-start | bytes 6291464 | tf_op jit(solution)/shard_map/ppermute | solution.py:58
  1.6 6.9 %collective-permute-start = (bf16[64,2048]{1,0:T(8,128)(2,1)S(1)}, bf16[64,2048]{1,0:T(8,128)(2,1)S(1)}, u32[]{:S(2)}, u32[]{:S(2)}) collective-permute-start(bf16[64,2048]{1,0:T(8,128)(2,1)S(1)} %get-tuple-element.20.refs_2_), channel_id=1, source_target_pairs={{0,1},{1,0},{2,3},{3,2},{4,5},{5,4},{6,7},{7,6},{8,9},{9,8},{10,11... | collective-permute-start | bytes 786440 | tf_op jit(solution)/shard_map/ppermute | solution.py:58
  4.2 16.3 %collective-permute-start.1 = (bf16[64,2048]{1,0:T(8,128)(2,1)S(1)}, bf16[64,2048]{1,0:T(8,128)(2,1)S(1)}, u32[]{:S(2)}, u32[]{:S(2)}) collective-permute-start(bf16[64,2048]{1,0:T(8,128)(2,1)S(1)} %get-tuple-element.21), channel_id=1, source_target_pairs={{0,1},{1,0},{2,3},{3,2},{4,5},{5,4},{6,7},{7,6},{8,9},{9,8},{10,11... | collective-permute-start | bytes 786440 | tf_op jit(solution)/shard_map/ppermute | solution.py:58
  8.5 12.0 %collective-permute-start.2 = (bf16[64,2048]{1,0:T(8,128)(2,1)S(1)}, bf16[64,2048]{1,0:T(8,128)(2,1)S(1)}, u32[]{:S(2)}, u32[]{:S(2)}) collective-permute-start(bf16[64,2048]{1,0:T(8,128)(2,1)S(1)} %collective-permute-done.refs_0_), channel_id=1, source_target_pairs={{0,20},{1,21},{2,22},{3,23},{4,16},{5,17},{6,18},{7,19},{8,28},{9,... | collective-permute-start | bytes 786440 | tf_op jit(solution)/shard_map/ppermute | solution.py:58
  9.9 4.5 %collective-permute-start.3 = (f32[16,128]{1,0:T(8,128)S(1)}, f32[16,128]{1,0:T(8,128)S(1)}, u32[]{:S(2)}, u32[]{:S(2)}) collective-permute-start(f32[16,128]{1,0:T(8,128)S(1)} %get-tuple-element.22.refs_2_), channel_id=1, source_target_pairs={{0,20},{1,21},{2,22},{3,23},{4,16},{5,17},{6,18},{7,19},{8,28},{9,... | collective-permute-start | bytes 24584 | tf_op jit(solution)/shard_map/ppermute | solution.py:58
  14.4 3.5 %collective-permute-start.4 = (f32[16,128]{1,0:T(8,128)S(1)}, f32[16,128]{1,0:T(8,128)S(1)}, u32[]{:S(2)}, u32[]{:S(2)}) collective-permute-start(f32[16,128]{1,0:T(8,128)S(1)} %collective-permute-done.3.refs_0_), channel_id=1, source_target_pairs={{0,20},{1,21},{2,22},{3,23},{4,16},{5,17},{6,18},{7,19},{8,28},{9,... | collective-permute-start | bytes 24584 | tf_op jit(solution)/shard_map/ppermute | solution.py:58
  23.5 2.1 %collective-permute-start.6 = (bf16[4,128,512]{2,1,0:T(8,128)(2,1)S(1)}, bf16[4,128,512]{2,1,0:T(8,128)(2,1)S(1)}, u32[]{:S(2)}, u32[]{:S(2)}) collective-permute-start(bf16[4,128,512]{2,1,0:T(8,128)(2,1)S(1)} %bitcast.7), channel_id=1, source_target_pairs={{0,16},{1,17},{2,18},{3,19},{4,20},{5,21},{6,22},{7,23},{8,24},{9,... | collective-permute-start | bytes 1572872 | tf_op jit(solution)/shard_map/ppermute | solution.py:58
  25.7 6.4 %collective-permute-start.7 = (bf16[2,128,512]{2,1,0:T(8,128)(2,1)S(1)}, bf16[2,128,512]{2,1,0:T(8,128)(2,1)S(1)}, u32[]{:S(2)}, u32[]{:S(2)}) collective-permute-start(bf16[2,128,512]{2,1,0:T(8,128)(2,1)S(1)} %get-tuple-element.32), channel_id=1, source_target_pairs={{0,2},{1,3},{2,0},{3,1},{4,6},{5,7},{6,4},{7,5},{8,10},{9,11},{10,... | collective-permute-start | bytes 786440 | tf_op jit(solution)/shard_map/ppermute | solution.py:58
  32.2 7.3 %collective-permute-start.8 = (bf16[1,128,512]{2,1,0:T(8,128)(2,1)S(1)}, bf16[1,128,512]{2,1,0:T(8,128)(2,1)S(1)}, u32[]{:S(2)}, u32[]{:S(2)}) collective-permute-start(bf16[1,128,512]{2,1,0:T(8,128)(2,1)S(1)} %get-tuple-element.34), channel_id=1, source_target_pairs={{0,8},{1,9},{2,10},{3,11},{4,12},{5,13},{6,14},{7,15},{8,0},{9,1},... | collective-permute-start | bytes 393224 | tf_op jit(solution)/shard_map/ppermute | solution.py:58
